TPU v7x, 32 devices: a whole 2x2x4 slice. The times are simulated.
32 devices in a mesh: row: 4 (over y, x), col: 8 (over z, core).
Axes of the slice: x: 2, y: 2, z: 4, core: 2. Of those that a mesh axis runs over, the one named last changes fastest.
Arguments:
- sim: bfloat16 [8192, 8192], P('row', 'col'), may hold values from -6 to 6
- diag_blocks: bfloat16 [2048, 8192], P(None, 'col'), may hold values from -0.125 to 0.125
- match_perm: int32 [4, 2048], replicated, may hold values from 0 to 2047, each once within a row
- match_scale: float32 [4, 2048], replicated, may hold values from 0.3 to 1.5
- features: bfloat16 [8192, 256], P('col'), may hold values from -0.0625 to 0.0625
Outputs:
- new_sim: bfloat16 [8192, 8192], P('row', 'col')
- aggregated: float32 [8192, 256], P(('row', 'col'))
Inputs may be any that keep to these rules, and one draw needn't show every extreme that they name: Each row of match_perm lists every number of 0 to 2047 once.
All inputs are finite; a program needn't handle non-finite values.
Results may differ from a plain program's by a relative error of at most 0.0058.
Values may be sent and summed in bfloat16 or wider, within the bound.
No kernel may reach another device: no remote copies, remote signals or barrier semaphores. Data moves between devices by JAX's collectives and lax.ppermute only.
A program may use at most 128 MiB of HBM per device.

v0:
```python
import jax
import jax.numpy as jnp
from jax import lax
from jax.experimental import pallas as pl
from jax.experimental.pallas import tpu as pltpu
from jax.sharding import PartitionSpec as P


decay_factor = 0.8
parts = (2,) * 8
groups = ((0, 6),)
first_quarters = 3
pieces = 2


def flipped(value, axis, mask):
    pairs = [(source, source ^ mask) for source in range(lax.axis_size(axis))]
    return lax.ppermute(value, axis, pairs)


def shifted(value, axis, steps):
    count = lax.axis_size(axis)
    pairs = [(source, (source + steps) % count) for source in range(count)]
    return lax.ppermute(value, axis, pairs)


def dot(a, b):
    return jnp.dot(a, b, preferred_element_type=jnp.float32)


def dot_t(a, b):
    return lax.dot_general(a, b, (((0,), (0,)), ((), ())), preferred_element_type=jnp.float32)


def one_hot(start, rows, targets):
    index = start + lax.broadcasted_iota(jnp.int32, (rows, targets.shape[0]), 0)
    return (index == targets[None, :]).astype(jnp.bfloat16)


def part(x, start, size, axis=0):
    return lax.dynamic_slice_in_dim(x, start, size, axis)


def pick(items, index):
    result = items[0]
    for position in range(1, len(items)):
        result = jnp.where(index == position, items[position], result)
    return result


def tile_product(refs, kept, h, start):
    b_own, b_par, perm, scale = refs
    near, far = kept
    shape = (perm.shape[1], near.shape[0])
    index = start + lax.broadcasted_iota(jnp.int32, shape, 1)
    chosen = (index == perm[0]).astype(jnp.bfloat16)
    moved = dot(chosen, far[...]) * scale[0]
    return moved + dot_t(jnp.where(h == 0, b_own[...], b_par[...]), near[...])


def keep(chunks, kept):
    @pl.when((pl.program_id(0) == 0) & (pl.program_id(1) == 0))
    def _():
        start = 0
        for pair in chunks:
            depth = pair[0].shape[0]
            for one, whole in zip(pair, kept):
                whole[start : start + depth] = one[...]
            start += depth


def tile_specs(start, depth, chunks, tile, tiles, at):
    wide = chunks[0][0].shape[1]
    last = at(tiles - 1)
    specs = [
        pl.BlockSpec((depth, tile), lambda h, i, *_: (start // depth, jnp.where(h == 0, at(i), last))),
        pl.BlockSpec((depth, tile), lambda h, i, *_: (start // depth, jnp.where(h == 0, at(0), at(i)))),
        pl.BlockSpec((1, tile, 1), lambda h, i, *_: (h, at(i), 0)),
        pl.BlockSpec((1, tile, 1), lambda h, i, *_: (h, at(i), 0)),
    ]
    for near, _ in chunks:
        specs += [pl.BlockSpec((near.shape[0], wide), lambda h, i, *_: (0, 0))] * 2
    return specs


def paired(refs, count):
    return [(refs[2 * n], refs[2 * n + 1]) for n in range(count)]


def flat(chunks):
    return [one for pair in chunks for one in pair]


def accumulate(halves, perm, scale, chunks, start, total, dtype=jnp.float32):
    tall = halves[0].shape[1]
    wide = chunks[0][0].shape[1]
    depth = sum(near.shape[0] for near, _ in chunks)
    tile = min(512, tall)
    count = len(chunks)

    def body(*refs):
        kept = refs[-2:]
        out = refs[-3]
        keep(paired(refs[4:], count), kept)
        result = tile_product(refs[:4], kept, pl.program_id(0), start)
        if total is not None:
            result = result + refs[-4][0]
        out[0] = result.astype(dtype)

    place = pl.BlockSpec((1, tile, wide), lambda h, i: (h, i, 0))
    specs = tile_specs(start, depth, chunks, tile, tall // tile, lambda i: i)
    operands = [*halves, perm, scale, *flat(chunks)]
    if total is not None:
        specs.append(place)
        operands.append(total)
    return pl.pallas_call(
        body,
        out_shape=jax.ShapeDtypeStruct((2, tall, wide), dtype),
        grid=(2, tall // tile),
        in_specs=specs,
        out_specs=place,
        scratch_shapes=[pltpu.VMEM((depth, wide), jnp.bfloat16)] * 2,
        input_output_aliases={} if total is None else {len(operands) - 1: 0},
        compiler_params=pltpu.CompilerParams(vmem_limit_bytes=58 * 2**20),
        name="accumulate",
    )(*operands)


def finish(halves, perm, scale, chunks, start, total, late, arrived, factors, features, origin):
    _, tall, wide = total.shape
    depth = sum(near.shape[0] for near, _ in chunks)
    tile = min(512, tall)
    tiles = tall // tile
    count = len(chunks)
    thin = late[0].shape[2]
    width = features.shape[1]

    def body(origin_ref, *refs):
        h = pl.program_id(0)
        keep(paired(refs[4:], count), refs[-2:])
        others = refs[4 + 2 * count :]
        total_ref, here, here_par, there, there_par = others[:5]
        b_own, b_par, perm_c, scale_c, feature_ref, sim_ref, sum_ref = others[5:12]
        index = lax.broadcasted_iota(jnp.int32, (thin, wide), 0)
        g_own = (index + origin_ref[3] == perm_c[...]).astype(jnp.bfloat16)
        g_par = (index + origin_ref[4] == perm_c[...]).astype(jnp.bfloat16)
        moved = dot(there[0], g_own) + dot(there_par[0], g_par)
        result = total_ref[0] + moved * scale_c[...]
        result = result + dot(here[0], b_own[...]) + dot(here_par[0], b_par[...])
        result = result + tile_product(refs[:4], refs[-2:], h, start)
        place = jnp.where(h == 0, origin_ref[0], 1 - origin_ref[0])
        row = origin_ref[1] + place * tall + pl.program_id(1) * tile
        row = row + lax.broadcasted_iota(jnp.int32, result.shape, 0)
        col = origin_ref[2] + lax.broadcasted_iota(jnp.int32, result.shape, 1)
        done = jnp.where(row == col, 1.0, decay_factor * result).astype(jnp.bfloat16)
        sim_ref[...] = done
        sum_ref[...] = dot(done, feature_ref[...])

    def placed(h, i, o):
        return (jnp.where(h == 0, o[0], 1 - o[0]) * tiles + i, 0)

    same = pl.BlockSpec((1, tile, thin), lambda h, i, o: (h, i, 0))
    swapped = pl.BlockSpec((1, tile, thin), lambda h, i, o: (1 - h, i, 0))
    specs = tile_specs(start, depth, chunks, tile, tiles, lambda i: i)
    specs += [pl.BlockSpec((1, tile, wide), lambda h, i, o: (h, i, 0))]
    specs += [same, swapped, same, swapped]
    fixed = [*factors, features]
    specs += [pl.BlockSpec(one.shape, lambda h, i, o: (0, 0)) for one in fixed]
    return pl.pallas_call(
        body,
        out_shape=(
            jax.ShapeDtypeStruct((2 * tall, wide), jnp.bfloat16),
            jax.ShapeDtypeStruct((2 * tall, width), jnp.float32),
        ),
        grid_spec=pltpu.PrefetchScalarGridSpec(
            num_scalar_prefetch=1,
            grid=(2, tiles),
            in_specs=specs,
            out_specs=(pl.BlockSpec((tile, wide), placed), pl.BlockSpec((tile, width), placed)),
            scratch_shapes=[pltpu.VMEM((depth, wide), jnp.bfloat16)] * 2,
        ),
        compiler_params=pltpu.CompilerParams(vmem_limit_bytes=58 * 2**20),
        name="finish",
    )(origin, *halves, perm, scale, *flat(chunks), total, *late, *arrived, *fixed)


def gathered_block(diag_blocks, row_id, block_id, row_count, block_count):
    cols = 2 * block_count
    slice_rows = diag_blocks.shape[0] // row_count
    depth = slice_rows // pieces
    whole = jnp.zeros(diag_blocks.shape, diag_blocks.dtype)
    placed = []
    for n in range(pieces):
        own = part(diag_blocks, row_id * slice_rows + n * depth, depth)
        ups, downs = [own], [own]
        for step in range(1, block_count):
            up_pairs = [(c, c + 2) for c in range(cols - 2) if c // 2 >= step - 1]
            down_pairs = [(c, c - 2) for c in range(2, cols) if c // 2 + step - 1 <= block_count - 1]
            ups.append(lax.ppermute(ups[-1], "col", up_pairs))
            downs.append(lax.ppermute(downs[-1], "col", down_pairs))
        slices = [own] + [ups[j] + downs[block_count - j] for j in range(1, block_count)]
        for distance in range(row_count):
            wanted = row_id ^ distance
            piece = pick(slices, (block_id - wanted) % block_count)
            if distance:
                piece = flipped(piece, "row", distance)
            placed.append((distance, n, piece, wanted * slice_rows + n * depth))
    for _, _, piece, place in sorted(placed, key=lambda entry: entry[0] > 0):
        whole = lax.dynamic_update_slice_in_dim(whole, piece, place, 0)
    return whole


def program(sim, diag_blocks, match_perm, match_scale, features):
    row_count = lax.axis_size("row")
    col_count = lax.axis_size("col")
    block_count = col_count // 2
    row_id = lax.axis_index("row")
    col_id = lax.axis_index("col")
    block_id = col_id // 2
    side = col_id % 2
    rows, half = sim.shape
    other = 1 - side
    bf16 = jnp.bfloat16
    first = half * first_quarters // 4
    spans = [(sum(parts[:n]) * rows // 16, parts[n] * rows // 16) for n in range(len(parts))]

    whole_b = gathered_block(diag_blocks, row_id, block_id, row_count, block_count)
    late_here = sim[:, first:]
    late_far_rows = shifted(late_here, "row", row_count // 2)
    partner = flipped(sim, "col", 1)

    far_block = (block_id + block_count // 2) % block_count
    far_row = (row_id + row_count // 2) % row_count
    perm_c = part(lax.dynamic_index_in_dim(match_perm, far_block, 0, False), side * half, half)
    scale_c = part(lax.dynamic_index_in_dim(match_scale, far_block, 0, False), side * half, half)
    perm_r = lax.dynamic_index_in_dim(match_perm, far_row, 0, False)
    scale_r = lax.dynamic_index_in_dim(match_scale, far_row, 0, False)
    perm_r = jnp.stack([part(perm_r, side * half, half), part(perm_r, other * half, half)])
    scale_r = jnp.stack([part(scale_r, side * half, half), part(scale_r, other * half, half)])
    pick_own = one_hot(side * half, half, perm_c)
    pick_par = one_hot(other * half, half, perm_c)
    pick_own, pick_par = pick_own[:first], pick_par[:first]
    scale_rows = jnp.broadcast_to(scale_c[None, :], (max(d for _, d in spans), half))
    perm_r = perm_r[:, :, None]
    scale_r = scale_r[:, :, None]
    b_own = part(diag_blocks, side * half, half)
    b_par = part(diag_blocks, other * half, half)

    local = dot(sim[:, :first], b_own[:first])
    local = local + dot(partner[:, :first], b_par[:first])
    cuts = [sim[start : start + depth, :first] for start, depth in spans]
    chunks = []
    for n, (start, depth) in enumerate(spans):
        span = slice(start, start + depth)
        got = shifted(cuts[n], "col", col_count // 2)
        got_par = flipped(got, "col", 1)
        moved = dot(got, pick_own) + dot(got_par, pick_par)
        mixed = (local[span] + moved * scale_rows[:depth]).astype(bf16)
        chunks.append((mixed, shifted(mixed, "row", row_count // 2)))

    other_b = flipped(whole_b, "col", 1)
    halves = (whole_b, other_b)
    pair = [(late_here, late_far_rows)]
    late = accumulate(halves, perm_r, scale_r, pair, 0, None, bf16)
    there = shifted(late, "col", col_count // 2)
    late = (late, flipped(late, "col", 1))
    arrived = (there, flipped(there, "col", 1))
    total = None
    for low, high in groups:
        total = accumulate(
            halves, perm_r, scale_r, chunks[low:high], spans[low][0], total
        )

    origin = [side, row_id * rows, col_id * half, side * half + first, other * half + first]
    origin = jnp.stack(origin).astype(jnp.int32)
    factors = (b_own[first:], b_par[first:], perm_c[None, :], scale_c[None, :])
    low = groups[-1][1]
    new_sim, sums = finish(
        halves, perm_r, scale_r, chunks[low:], spans[low][0], total, late, arrived,
        factors, features, origin,
    )
    aggregated = scattered(sums, side, block_id, block_count)
    return new_sim, aggregated


def scattered(total, side, block_id, block_count):
    total = total.reshape(block_count, 2, -1, total.shape[1])
    kept = lax.dynamic_index_in_dim(total, side, 1, False)
    sent = lax.dynamic_index_in_dim(total, 1 - side, 1, False).astype(jnp.bfloat16)
    kept = kept + flipped(sent, "col", 1)
    result = lax.dynamic_index_in_dim(kept, block_id, 0, False)
    for distance in range(1, block_count):
        sent = lax.dynamic_index_in_dim(kept, block_id ^ distance, 0, False)
        result = result + flipped(sent.astype(jnp.bfloat16), "col", 2 * distance)
    return result


def solution(mesh):
    placed = (P("row", "col"), P(None, "col"), P(), P(), P("col", None))
    return jax.shard_map(
        program,
        mesh=mesh,
        in_specs=placed,
        out_specs=(P("row", "col"), P(("row", "col"), None)),
        check_vma=False,
    )
```

profile of v0, /device:TPU:0, one launch (start us, length us, event | category | flops | bytes accessed | tf_op | source)
XLA Modules:
  0.0 395.2 jit_solution(1094137095203532632)
XLA Ops:
  0.7 2.7 constant_dynamic-slice_fusion
  4.7 5.6 %collective-permute-start = (bf16[256,1024]{1,0:T(8,128)(2,1)S(1)}, bf16[256,1024]{1,0:T(8,128)(2,1)S(1)}, u32[]{:S(2)}, u32[]{:S(2)}) collective-permute-start(bf16[256,1024]{1,0:T(8,128)(2,1)S(1)} %get-tuple-element.16), channel_id=1, source_target_pairs={{0,2},{1,3},{2,4},{3,5},{4,6},{5,7},{8,10},{9,11},{10,12},{11,13},... | collective-permute-start | bytes 1572872 | tf_op jit(solution)/shard_map/ppermute | solution.py:199
  11.6 4.6 %collective-permute-start.6 = (bf16[256,1024]{1,0:T(8,128)(2,1)S(1)}, bf16[256,1024]{1,0:T(8,128)(2,1)S(1)}, u32[]{:S(2)}, u32[]{:S(2)}) collective-permute-start(bf16[256,1024]{1,0:T(8,128)(2,1)S(1)} %get-tuple-element.15), channel_id=1, source_target_pairs={{0,2},{1,3},{2,4},{3,5},{4,6},{5,7},{8,10},{9,11},{10,12},{11,13},... | collective-permute-start | bytes 1572872 | tf_op jit(solution)/shard_map/ppermute | solution.py:199
  16.2 4.9 %collective-permute-done.3 = bf16[256,1024]{1,0:T(8,128)(2,1)S(1)} collective-permute-done((bf16[256,1024]{1,0:T(8,128)(2,1)S(1)}, bf16[256,1024]{1,0:T(8,128)(2,1)S(1)}, u32[]{:S(2)}, u32[]{:S(2)}) %collective-permute-start.3) | collective-permute-done | bytes 524320 | tf_op jit(solution)/shard_map/ppermute | solution.py:200
  22.6 1.5 collective-permute-start.1
  24.1 8.3 %collective-permute-done.9 = bf16[256,1024]{1,0:T(8,128)(2,1)S(1)} collective-permute-done((bf16[256,1024]{1,0:T(8,128)(2,1)S(1)}, bf16[256,1024]{1,0:T(8,128)(2,1)S(1)}, u32[]{:S(2)}, u32[]{:S(2)}) %collective-permute-start.9) | collective-permute-done | bytes 524320 | tf_op jit(solution)/shard_map/ppermute | solution.py:200
  34.4 9.3 %collective-permute-done.4 = bf16[256,1024]{1,0:T(8,128)(2,1)} collective-permute-done((bf16[256,1024]{1,0:T(8,128)(2,1)S(1)}, bf16[256,1024]{1,0:T(8,128)(2,1)}, u32[]{:S(2)}, u32[]{:S(2)}) %collective-permute-start.4) | collective-permute-done | bytes 524320 | tf_op jit(solution)/shard_map/ppermute | solution.py:200
  45.7 9.2 %fusion.33 = f32[1024,2048]{0,1:T(8,128)} fusion(bf16[2048,1024]{1,0:T(8,128)(2,1)} %param.5, bf16[2048,1024]{1,0:T(8,128)(2,1)} %param.6, s32[]{:T(128)S(6)} %select_n.294), kind=kOutput, calls=%fused_computation.34 | convolution fusion | flops 3221225472 | bytes 13107204 | tf_op jit(solution)/shard_map/dot_general | solution.py:28
  57.0 9.0 %collective-permute-done.5 = bf16[256,1024]{1,0:T(8,128)(2,1)S(1)} collective-permute-done((bf16[256,1024]{1,0:T(8,128)(2,1)}, bf16[256,1024]{1,0:T(8,128)(2,1)S(1)}, u32[]{:S(2)}, u32[]{:S(2)}) %collective-permute-start.5) | collective-permute-done | bytes 524320 | tf_op jit(solution)/shard_map/ppermute | solution.py:200
  66.1 1.6 select_select_fusion.3
  67.6 2.6 broadcast_in_dim.10
  70.2 1.7 select_select_fusion.4
  71.9 1.9 collective-permute-start.12
  73.8 1.5 collective-permute-start.13
  76.5 2.6 collective-permute-start.14
  81.1 3.5 fusion.197
  84.6 2.3 collective-permute-done.12
  87.0 1.9 collective-permute-start.16
  89.9 7.9 %collective-permute-done.13 = bf16[256,1024]{1,0:T(8,128)(2,1)} collective-permute-done((bf16[256,1024]{1,0:T(8,128)(2,1)}, bf16[256,1024]{1,0:T(8,128)(2,1)}, u32[]{:S(2)}, u32[]{:S(2)}) %collective-permute-start.13) | collective-permute-done | bytes 524320 | tf_op jit(solution)/shard_map/ppermute | solution.py:18
  98.5 1.9 constant_dynamic-update-slice_fusion.5
  100.4 1.9 constant_dynamic-update-slice_fusion.4
  102.3 4.9 %collective-permute-start.20 = (bf16[256,768]{1,0:T(8,128)(2,1)}, bf16[256,768]{1,0:T(8,128)(2,1)}, u32[]{:S(2)}, u32[]{:S(2)}) collective-permute-start(bf16[256,768]{1,0:T(8,128)(2,1)} %get-tuple-element.25), channel_id=1, source_target_pairs={{0,4},{1,5},{2,6},{3,7},{4,0},{5,1},{6,2},{7,3},{8,12},{9,13},{10,... | collective-permute-start | bytes 1179656 | tf_op jit(solution)/shard_map/ppermute | solution.py:24
  107.2 1.9 constant_dynamic-update-slice_fusion.3
  109.4 4.6 %collective-permute-start.23 = (bf16[256,768]{1,0:T(8,128)(2,1)}, bf16[256,768]{1,0:T(8,128)(2,1)}, u32[]{:S(2)}, u32[]{:S(2)}) collective-permute-start(bf16[256,768]{1,0:T(8,128)(2,1)} %get-tuple-element.24), channel_id=1, source_target_pairs={{0,4},{1,5},{2,6},{3,7},{4,0},{5,1},{6,2},{7,3},{8,12},{9,13},{10,... | collective-permute-start | bytes 1179656 | tf_op jit(solution)/shard_map/ppermute | solution.py:24
  114.8 4.3 %collective-permute-done.16 = bf16[256,1024]{1,0:T(8,128)(2,1)S(1)} collective-permute-done((bf16[256,1024]{1,0:T(8,128)(2,1)S(1)}, bf16[256,1024]{1,0:T(8,128)(2,1)S(1)}, u32[]{:S(2)}, u32[]{:S(2)}) %collective-permute-start.16) | collective-permute-done | bytes 524320 | tf_op jit(solution)/shard_map/ppermute | solution.py:18
  119.1 3.6 collective-permute-start.26
  129.5 13.3 %collective-permute-done.20 = bf16[256,768]{1,0:T(8,128)(2,1)} collective-permute-done((bf16[256,768]{1,0:T(8,128)(2,1)}, bf16[256,768]{1,0:T(8,128)(2,1)}, u32[]{:S(2)}, u32[]{:S(2)}) %collective-permute-start.20) | collective-permute-done | bytes 393248 | tf_op jit(solution)/shard_map/ppermute | solution.py:24
  142.7 1.8 fusion.28
  144.5 15.1 %collective-permute-done.23 = bf16[256,768]{1,0:T(8,128)(2,1)} collective-permute-done((bf16[256,768]{1,0:T(8,128)(2,1)}, bf16[256,768]{1,0:T(8,128)(2,1)}, u32[]{:S(2)}, u32[]{:S(2)}) %collective-permute-start.23) | collective-permute-done | bytes 393248 | tf_op jit(solution)/shard_map/ppermute | solution.py:24
  159.6 2.9 fusion.26
  162.5 13.9 %collective-permute-done.26 = bf16[256,768]{1,0:T(8,128)(2,1)} collective-permute-done((bf16[256,768]{1,0:T(8,128)(2,1)}, bf16[256,768]{1,0:T(8,128)(2,1)}, u32[]{:S(2)}, u32[]{:S(2)}) %collective-permute-start.26) | collective-permute-done | bytes 393248 | tf_op jit(solution)/shard_map/ppermute | solution.py:24
  176.5 1.8 fusion.24
  178.2 15.0 %collective-permute-done.29 = bf16[256,768]{1,0:T(8,128)(2,1)S(1)} collective-permute-done((bf16[256,768]{1,0:T(8,128)(2,1)}, bf16[256,768]{1,0:T(8,128)(2,1)S(1)}, u32[]{:S(2)}, u32[]{:S(2)}) %collective-permute-start.29) | collective-permute-done | bytes 393248 | tf_op jit(solution)/shard_map/ppermute | solution.py:24
  193.2 1.8 fusion.22
  195.0 15.0 %collective-permute-done.32 = bf16[256,768]{1,0:T(8,128)(2,1)S(1)} collective-permute-done((bf16[256,768]{1,0:T(8,128)(2,1)S(1)}, bf16[256,768]{1,0:T(8,128)(2,1)S(1)}, u32[]{:S(2)}, u32[]{:S(2)}) %collective-permute-start.32) | collective-permute-done | bytes 393248 | tf_op jit(solution)/shard_map/ppermute | solution.py:24
  210.1 1.8 fusion.20
  211.8 11.0 %collective-permute-done.35 = bf16[256,768]{1,0:T(8,128)(2,1)} collective-permute-done((bf16[256,768]{1,0:T(8,128)(2,1)S(1)}, bf16[256,768]{1,0:T(8,128)(2,1)}, u32[]{:S(2)}, u32[]{:S(2)}) %collective-permute-start.35) | collective-permute-done | bytes 393248 | tf_op jit(solution)/shard_map/ppermute | solution.py:24
  222.8 1.4 collective-permute-start.44
  224.2 2.8 fusion.18
  227.0 3.4 collective-permute-done.38
  230.4 2.7 fusion.16
  234.5 1.8 fusion.30
  236.8 6.1 %add_bitcast_fusion = f32[2048,1024]{1,0:T(8,128)S(1)} fusion(f32[1024,2048]{0,1:T(8,128)S(1)} %bitcast.143, bf16[2048,1024]{1,0:T(8,128)(2,1)} %collective-permute-done.19, bf16[2048,1024]{1,0:T(8,128)(2,1)} %param.6, s32[]{:T(128)S(6)} %select_n.296), kind=kOutput, calls=%fused_computation.32 | convolution fusion | flops 3223322624 | bytes 21495812 | tf_op jit(solution)/shard_map/dot_general | solution.py:28
  243.1 2.1 fusion.183.refs_4_
  247.6 9.7 %accumulate.3.refs_9_ = bf16[2,1024,256]{2,1,0:T(8,128)(2,1)} custom-call(bf16[2048,1024]{1,0:T(8,128)(2,1)} %constant_dynamic-update-slice_fusion.refs_0_, bf16[2048,1024]{1,0:T(8,128)(2,1)} %collective-permute-done.18.refs_1_, s32[2,1024,1]{2,1,0:T(8,128)} %copy.48.refs_2_, f32[2,1024,1]{2,1,0:T(8,128)} %copy.49.refs_3_, bf16[2048,256]{1,0:T(8,128)(2,1)} %copy-done.1, ...), custom_call_target="tpu_custom_call" | custom-call | tf_op jit(solution)/shard_map/accumulate/pallas_call | solution.py:116
  257.3 2.4 fusion.174.refs_6_
  259.9 2.6 fusion.171.refs_8_
  264.6 2.0 fusion.168.refs_10_
  266.6 2.4 fusion.165.refs_12_
  271.1 6.2 %collective-permute-done.28.refs_5_ = bf16[256,1024]{1,0:T(8,128)(2,1)S(1)} collective-permute-done((bf16[256,1024]{1,0:T(8,128)(2,1)S(1)}, bf16[256,1024]{1,0:T(8,128)(2,1)S(1)}, u32[]{:S(2)}, u32[]{:S(2)}) %collective-permute-start.28) | collective-permute-done | bytes 524320 | tf_op jit(solution)/shard_map/ppermute | solution.py:24
  278.6 10.0 %collective-permute-done.31.refs_7_ = bf16[256,1024]{1,0:T(8,128)(2,1)S(1)} collective-permute-done((bf16[256,1024]{1,0:T(8,128)(2,1)S(1)}, bf16[256,1024]{1,0:T(8,128)(2,1)S(1)}, u32[]{:S(2)}, u32[]{:S(2)}) %collective-permute-start.31) | collective-permute-done | bytes 524320 | tf_op jit(solution)/shard_map/ppermute | solution.py:24
  288.6 17.4 %collective-permute-done.46.refs_11_ = bf16[2,1024,256]{2,1,0:T(8,128)(2,1)S(1)} collective-permute-done((bf16[2,1024,256]{2,1,0:T(8,128)(2,1)}, bf16[2,1024,256]{2,1,0:T(8,128)(2,1)S(1)}, u32[]{:S(2)}, u32[]{:S(2)}) %collective-permute-start.46) | collective-permute-done | bytes 1048608 | tf_op jit(solution)/shard_map/ppermute | solution.py:24
  306.0 3.2 fusion.180.refs_6_
  309.2 2.9 fusion.186.refs_14_
  314.3 7.9 %collective-permute-done.40.refs_13_ = bf16[256,1024]{1,0:T(8,128)(2,1)S(1)} collective-permute-done((bf16[256,1024]{1,0:T(8,128)(2,1)S(1)}, bf16[256,1024]{1,0:T(8,128)(2,1)S(1)}, u32[]{:S(2)}, u32[]{:S(2)}) %collective-permute-start.40) | collective-permute-done | bytes 524320 | tf_op jit(solution)/shard_map/ppermute | solution.py:24
  325.0 8.6 %collective-permute-done.43.refs_15_ = bf16[256,1024]{1,0:T(8,128)(2,1)} collective-permute-done((bf16[256,1024]{1,0:T(8,128)(2,1)}, bf16[256,1024]{1,0:T(8,128)(2,1)}, u32[]{:S(2)}, u32[]{:S(2)}) %collective-permute-start.43) | collective-permute-done | bytes 524320 | tf_op jit(solution)/shard_map/ppermute | solution.py:24
  333.6 19.8 %accumulate.2.refs_8_ = f32[2,1024,1024]{2,1,0:T(8,128)} custom-call(bf16[2048,1024]{1,0:T(8,128)(2,1)} %constant_dynamic-update-slice_fusion.refs_0_, bf16[2048,1024]{1,0:T(8,128)(2,1)} %collective-permute-done.18.refs_1_, s32[2,1024,1]{2,1,0:T(8,128)} %copy.48.refs_2_, f32[2,1024,1]{2,1,0:T(8,128)} %copy.49.refs_3_, bf16[256,1024]{1,0:T(8,128)(2,1)} %copy-done.6, ...), custom_call_target="tpu_custom_call" | custom-call | tf_op jit(solution)/shard_map/accumulate/pallas_call | solution.py:116
  353.4 1.9 collective-permute-done.25.refs_7_
  356.4 17.4 %finish.1 = (bf16[2048,1024]{1,0:T(8,128)(2,1)}, f32[2048,256]{1,0:T(8,128)}) custom-call(s32[5]{0:T(128)} %stack.33.origin_ref, bf16[2048,1024]{1,0:T(8,128)(2,1)} %constant_dynamic-update-slice_fusion.refs_0_, bf16[2048,1024]{1,0:T(8,128)(2,1)} %collective-permute-done.18.refs_1_, s32[2,1024,1]{2,1,0:T(8,128)} %copy.48.refs_2_, ...), custom_call_target="tpu_custom_call" | custom-call | tf_op jit(solution)/shard_map/finish/pallas_call | solution.py:169
  375.3 1.9 collective-permute-done.48
  378.6 3.4 collective-permute-start.51
  381.9 1.9 collective-permute-start.50
  383.9 2.6 collective-permute-done.51
  386.5 7.9 %collective-permute-done.50 = bf16[256,256]{1,0:T(8,128)(2,1)S(1)} collective-permute-done((bf16[256,256]{1,0:T(8,128)(2,1)S(1)}, bf16[256,256]{1,0:T(8,128)(2,1)S(1)}, u32[]{:S(2)}, u32[]{:S(2)}) %collective-permute-start.50) | collective-permute-done | bytes 131104 | tf_op jit(solution)/shard_map/ppermute | solution.py:18
  (145 shorter events, 42.3 us)
Async XLA Ops:
  3.4 17.7 %collective-permute-start.3 = (bf16[256,1024]{1,0:T(8,128)(2,1)S(1)}, bf16[256,1024]{1,0:T(8,128)(2,1)S(1)}, u32[]{:S(2)}, u32[]{:S(2)}) collective-permute-start(bf16[256,1024]{1,0:T(8,128)(2,1)S(1)} %get-tuple-element.16), channel_id=1, source_target_pairs={{2,0},{3,1},{4,2},{5,3},{6,4},{7,5},{10,8},{11,9},{12,10},{13,11},... | collective-permute-start | bytes 1572872 | tf_op jit(solution)/shard_map/ppermute | solution.py:200
  4.7 17.9 %collective-permute-start = (bf16[256,1024]{1,0:T(8,128)(2,1)S(1)}, bf16[256,1024]{1,0:T(8,128)(2,1)S(1)}, u32[]{:S(2)}, u32[]{:S(2)}) collective-permute-start(bf16[256,1024]{1,0:T(8,128)(2,1)S(1)} %get-tuple-element.16), channel_id=1, source_target_pairs={{0,2},{1,3},{2,4},{3,5},{4,6},{5,7},{8,10},{9,11},{10,12},{11,13},... | collective-permute-start | bytes 1572872 | tf_op jit(solution)/shard_map/ppermute | solution.py:199
  10.3 22.0 %collective-permute-start.9 = (bf16[256,1024]{1,0:T(8,128)(2,1)S(1)}, bf16[256,1024]{1,0:T(8,128)(2,1)S(1)}, u32[]{:S(2)}, u32[]{:S(2)}) collective-permute-start(bf16[256,1024]{1,0:T(8,128)(2,1)S(1)} %get-tuple-element.15), channel_id=1, source_target_pairs={{2,0},{3,1},{4,2},{5,3},{6,4},{7,5},{10,8},{11,9},{12,10},{13,11},... | collective-permute-start | bytes 1572872 | tf_op jit(solution)/shard_map/ppermute | solution.py:200
  11.6 22.0 %collective-permute-start.6 = (bf16[256,1024]{1,0:T(8,128)(2,1)S(1)}, bf16[256,1024]{1,0:T(8,128)(2,1)S(1)}, u32[]{:S(2)}, u32[]{:S(2)}) collective-permute-start(bf16[256,1024]{1,0:T(8,128)(2,1)S(1)} %get-tuple-element.15), channel_id=1, source_target_pairs={{0,2},{1,3},{2,4},{3,5},{4,6},{5,7},{8,10},{9,11},{10,12},{11,13},... | collective-permute-start | bytes 1572872 | tf_op jit(solution)/shard_map/ppermute | solution.py:199
  21.1 22.6 %collective-permute-start.4 = (bf16[256,1024]{1,0:T(8,128)(2,1)S(1)}, bf16[256,1024]{1,0:T(8,128)(2,1)}, u32[]{:S(2)}, u32[]{:S(2)}) collective-permute-start(bf16[256,1024]{1,0:T(8,128)(2,1)S(1)} %collective-permute-done.3), channel_id=1, source_target_pairs={{2,0},{3,1},{4,2},{5,3},{10,8},{11,9},{12,10},{13,11},{18,16},{19,... | collective-permute-start | bytes 1572872 | tf_op jit(solution)/shard_map/ppermute | solution.py:200
  22.6 22.4 %collective-permute-start.1 = (bf16[256,1024]{1,0:T(8,128)(2,1)S(1)}, bf16[256,1024]{1,0:T(8,128)(2,1)}, u32[]{:S(2)}, u32[]{:S(2)}) collective-permute-start(bf16[256,1024]{1,0:T(8,128)(2,1)S(1)} %collective-permute-done), channel_id=1, source_target_pairs={{2,4},{3,5},{4,6},{5,7},{10,12},{11,13},{12,14},{13,15},{18,20},{1... | collective-permute-start | bytes 1572872 | tf_op jit(solution)/shard_map/ppermute | solution.py:199
  24.1 212.3 %collective-permute-start.19 = (bf16[2048,1024]{1,0:T(8,128)(2,1)}, bf16[2048,1024]{1,0:T(8,128)(2,1)}, u32[]{:S(2)}, u32[]{:S(2)}) collective-permute-start(bf16[2048,1024]{1,0:T(8,128)(2,1)} %param.5), channel_id=1, source_target_pairs={{0,1},{1,0},{2,3},{3,2},{4,5},{5,4},{6,7},{7,6},{8,9},{9,8},{10,11... | collective-permute-start | bytes 12582920 | tf_op jit(solution)/shard_map/ppermute | solution.py:18
  32.4 22.5 %collective-permute-start.10 = (bf16[256,1024]{1,0:T(8,128)(2,1)S(1)}, bf16[256,1024]{1,0:T(8,128)(2,1)S(1)}, u32[]{:S(2)}, u32[]{:S(2)}) collective-permute-start(bf16[256,1024]{1,0:T(8,128)(2,1)S(1)} %collective-permute-done.9), channel_id=1, source_target_pairs={{2,0},{3,1},{4,2},{5,3},{10,8},{11,9},{12,10},{13,11},{18,16},{19,... | collective-permute-start | bytes 1572872 | tf_op jit(solution)/shard_map/ppermute | solution.py:200
  33.7 22.5 %collective-permute-start.7 = (bf16[256,1024]{1,0:T(8,128)(2,1)S(1)}, bf16[256,1024]{1,0:T(8,128)(2,1)S(1)}, u32[]{:S(2)}, u32[]{:S(2)}) collective-permute-start(bf16[256,1024]{1,0:T(8,128)(2,1)S(1)} %collective-permute-done.6), channel_id=1, source_target_pairs={{2,4},{3,5},{4,6},{5,7},{10,12},{11,13},{12,14},{13,15},{18,20},{1... | collective-permute-start | bytes 1572872 | tf_op jit(solution)/shard_map/ppermute | solution.py:199
  43.7 22.4 %collective-permute-start.5 = (bf16[256,1024]{1,0:T(8,128)(2,1)}, bf16[256,1024]{1,0:T(8,128)(2,1)S(1)}, u32[]{:S(2)}, u32[]{:S(2)}) collective-permute-start(bf16[256,1024]{1,0:T(8,128)(2,1)} %collective-permute-done.4), channel_id=1, source_target_pairs={{2,0},{3,1},{10,8},{11,9},{18,16},{19,17},{26,24},{27,25}} | collective-permute-start | bytes 1572872 | tf_op jit(solution)/shard_map/ppermute | solution.py:200
  45.0 21.1 %collective-permute-start.2 = (bf16[256,1024]{1,0:T(8,128)(2,1)}, bf16[256,1024]{1,0:T(8,128)(2,1)S(1)}, u32[]{:S(2)}, u32[]{:S(2)}) collective-permute-start(bf16[256,1024]{1,0:T(8,128)(2,1)} %collective-permute-done.1), channel_id=1, source_target_pairs={{4,6},{5,7},{12,14},{13,15},{20,22},{21,23},{28,30},{29,31}} | collective-permute-start | bytes 1572872 | tf_op jit(solution)/shard_map/ppermute | solution.py:199
  54.9 21.6 %collective-permute-start.11 = (bf16[256,1024]{1,0:T(8,128)(2,1)S(1)}, bf16[256,1024]{1,0:T(8,128)(2,1)S(1)}, u32[]{:S(2)}, u32[]{:S(2)}) collective-permute-start(bf16[256,1024]{1,0:T(8,128)(2,1)S(1)} %collective-permute-done.10), channel_id=1, source_target_pairs={{2,0},{3,1},{10,8},{11,9},{18,16},{19,17},{26,24},{27,25}} | collective-permute-start | bytes 1572872 | tf_op jit(solution)/shard_map/ppermute | solution.py:200
  56.2 22.9 %collective-permute-start.8 = (bf16[256,1024]{1,0:T(8,128)(2,1)S(1)}, bf16[256,1024]{1,0:T(8,128)(2,1)S(1)}, u32[]{:S(2)}, u32[]{:S(2)}) collective-permute-start(bf16[256,1024]{1,0:T(8,128)(2,1)S(1)} %collective-permute-done.7), channel_id=1, source_target_pairs={{4,6},{5,7},{12,14},{13,15},{20,22},{21,23},{28,30},{29,31}} | collective-permute-start | bytes 1572872 | tf_op jit(solution)/shard_map/ppermute | solution.py:199
  71.9 15.1 %collective-permute-start.12 = (bf16[256,1024]{1,0:T(8,128)(2,1)}, bf16[256,1024]{1,0:T(8,128)(2,1)}, u32[]{:S(2)}, u32[]{:S(2)}) collective-permute-start(bf16[256,1024]{1,0:T(8,128)(2,1)} %get-tuple-element.30), channel_id=1, source_target_pairs={{0,8},{8,0},{16,24},{24,16},{1,9},{9,1},{17,25},{25,17},{2,10},{10... | collective-permute-start | bytes 1572872 | tf_op jit(solution)/shard_map/ppermute | solution.py:18
  73.8 24.0 %collective-permute-start.13 = (bf16[256,1024]{1,0:T(8,128)(2,1)}, bf16[256,1024]{1,0:T(8,128)(2,1)}, u32[]{:S(2)}, u32[]{:S(2)}) collective-permute-start(bf16[256,1024]{1,0:T(8,128)(2,1)} %get-tuple-element.29), channel_id=1, source_target_pairs={{0,16},{8,24},{16,0},{24,8},{1,17},{9,25},{17,1},{25,9},{2,18},{10... | collective-permute-start | bytes 1572872 | tf_op jit(solution)/shard_map/ppermute | solution.py:18
  76.5 25.8 %collective-permute-start.14 = (bf16[256,1024]{1,0:T(8,128)(2,1)S(1)}, bf16[256,1024]{1,0:T(8,128)(2,1)}, u32[]{:S(2)}, u32[]{:S(2)}) collective-permute-start(bf16[256,1024]{1,0:T(8,128)(2,1)S(1)} %get-tuple-element.10), channel_id=1, source_target_pairs={{0,24},{8,16},{16,8},{24,0},{1,25},{9,17},{17,9},{25,1},{2,26},{10... | collective-permute-start | bytes 1572872 | tf_op jit(solution)/shard_map/ppermute | solution.py:18
  80.6 28.8 %collective-permute-start.15 = (bf16[256,1024]{1,0:T(8,128)(2,1)S(1)}, bf16[256,1024]{1,0:T(8,128)(2,1)S(1)}, u32[]{:S(2)}, u32[]{:S(2)}) collective-permute-start(bf16[256,1024]{1,0:T(8,128)(2,1)S(1)} %get-tuple-element.27), channel_id=1, source_target_pairs={{0,8},{8,0},{16,24},{24,16},{1,9},{9,1},{17,25},{25,17},{2,10},{10... | collective-permute-start | bytes 1572872 | tf_op jit(solution)/shard_map/ppermute | solution.py:18
  87.0 32.1 %collective-permute-start.16 = (bf16[256,1024]{1,0:T(8,128)(2,1)S(1)}, bf16[256,1024]{1,0:T(8,128)(2,1)S(1)}, u32[]{:S(2)}, u32[]{:S(2)}) collective-permute-start(bf16[256,1024]{1,0:T(8,128)(2,1)S(1)} %get-tuple-element.26), channel_id=1, source_target_pairs={{0,16},{8,24},{16,0},{24,8},{1,17},{9,25},{17,1},{25,9},{2,18},{10... | collective-permute-start | bytes 1572872 | tf_op jit(solution)/shard_map/ppermute | solution.py:18
  89.8 219.4 %copy-start.19 = (s32[1,1024]{1,0:T(1,128)}, s32[1,1024]{1,0:T(1,128)S(1)}, u32[]{:S(2)}) copy-start(s32[1,1024]{1,0:T(1,128)S(1)} %get-tuple-element.38.refs_15_) | copy-start | bytes 12292
  97.8 25.8 %collective-permute-start.17 = (bf16[256,1024]{1,0:T(8,128)(2,1)S(1)}, bf16[256,1024]{1,0:T(8,128)(2,1)S(1)}, u32[]{:S(2)}, u32[]{:S(2)}) collective-permute-start(bf16[256,1024]{1,0:T(8,128)(2,1)S(1)} %get-tuple-element.6), channel_id=1, source_target_pairs={{0,24},{8,16},{16,8},{24,0},{1,25},{9,17},{17,9},{25,1},{2,26},{10... | collective-permute-start | bytes 1572872 | tf_op jit(solution)/shard_map/ppermute | solution.py:18
  102.3 40.4 %collective-permute-start.20 = (bf16[256,768]{1,0:T(8,128)(2,1)}, bf16[256,768]{1,0:T(8,128)(2,1)}, u32[]{:S(2)}, u32[]{:S(2)}) collective-permute-start(bf16[256,768]{1,0:T(8,128)(2,1)} %get-tuple-element.25), channel_id=1, source_target_pairs={{0,4},{1,5},{2,6},{3,7},{4,0},{5,1},{6,2},{7,3},{8,12},{9,13},{10,... | collective-permute-start | bytes 1179656 | tf_op jit(solution)/shard_map/ppermute | solution.py:24
  109.4 50.2 %collective-permute-start.23 = (bf16[256,768]{1,0:T(8,128)(2,1)}, bf16[256,768]{1,0:T(8,128)(2,1)}, u32[]{:S(2)}, u32[]{:S(2)}) collective-permute-start(bf16[256,768]{1,0:T(8,128)(2,1)} %get-tuple-element.24), channel_id=1, source_target_pairs={{0,4},{1,5},{2,6},{3,7},{4,0},{5,1},{6,2},{7,3},{8,12},{9,13},{10,... | collective-permute-start | bytes 1179656 | tf_op jit(solution)/shard_map/ppermute | solution.py:24
  119.1 57.4 %collective-permute-start.26 = (bf16[256,768]{1,0:T(8,128)(2,1)}, bf16[256,768]{1,0:T(8,128)(2,1)}, u32[]{:S(2)}, u32[]{:S(2)}) collective-permute-start(bf16[256,768]{1,0:T(8,128)(2,1)} %get-tuple-element.23), channel_id=1, source_target_pairs={{0,4},{1,5},{2,6},{3,7},{4,0},{5,1},{6,2},{7,3},{8,12},{9,13},{10,... | collective-permute-start | bytes 1179656 | tf_op jit(solution)/shard_map/ppermute | solution.py:24
  124.4 122.3 %collective-permute-start.18 = (bf16[2048,1024]{1,0:T(8,128)(2,1)}, bf16[2048,1024]{1,0:T(8,128)(2,1)}, u32[]{:S(2)}, u32[]{:S(2)}) collective-permute-start(bf16[2048,1024]{1,0:T(8,128)(2,1)} %constant_dynamic-update-slice_fusion.refs_0_), channel_id=1, source_target_pairs={{0,1},{1,0},{2,3},{3,2},{4,5},{5,4},{6,7},{7,6},{8,9},{9,8},{10,11... | collective-permute-start | bytes 12582920 | tf_op jit(solution)/shard_map/ppermute | solution.py:18
  125.3 183.9 %copy-start.20 = (f32[1,1024]{1,0:T(1,128)}, f32[1,1024]{1,0:T(1,128)S(1)}, u32[]{:S(2)}) copy-start(f32[1,1024]{1,0:T(1,128)S(1)} %get-tuple-element.35.refs_16_) | copy-start | bytes 12292
  125.4 51.1 %copy-start.17 = (bf16[256,768]{1,0:T(8,128)(2,1)S(1)}, bf16[256,768]{1,0:T(8,128)(2,1)}, u32[]{:S(2)}) copy-start(bf16[256,768]{1,0:T(8,128)(2,1)} %get-tuple-element.20) | copy-start | bytes 1179652
  126.7 96.1 %copy-start.1 = (bf16[2048,256]{1,0:T(8,128)(2,1)}, bf16[2048,256]{1,0:T(8,128)(2,1)S(1)}, u32[]{:S(2)}) copy-start(bf16[2048,256]{1,0:T(8,128)(2,1)S(1)} %slice.97.refs_4_) | copy-start | bytes 3145732
  128.1 65.1 %copy-start.16 = (bf16[256,768]{1,0:T(8,128)(2,1)S(1)}, bf16[256,768]{1,0:T(8,128)(2,1)}, u32[]{:S(2)}) copy-start(bf16[256,768]{1,0:T(8,128)(2,1)} %get-tuple-element.19) | copy-start | bytes 1179652
  142.7 50.5 %collective-permute-start.29 = (bf16[256,768]{1,0:T(8,128)(2,1)}, bf16[256,768]{1,0:T(8,128)(2,1)S(1)}, u32[]{:S(2)}, u32[]{:S(2)}) collective-permute-start(bf16[256,768]{1,0:T(8,128)(2,1)} %get-tuple-element.22), channel_id=1, source_target_pairs={{0,4},{1,5},{2,6},{3,7},{4,0},{5,1},{6,2},{7,3},{8,12},{9,13},{10,... | collective-permute-start | bytes 1179656 | tf_op jit(solution)/shard_map/ppermute | solution.py:24
  159.6 50.5 %collective-permute-start.32 = (bf16[256,768]{1,0:T(8,128)(2,1)S(1)}, bf16[256,768]{1,0:T(8,128)(2,1)S(1)}, u32[]{:S(2)}, u32[]{:S(2)}) collective-permute-start(bf16[256,768]{1,0:T(8,128)(2,1)S(1)} %copy-done.18), channel_id=1, source_target_pairs={{0,4},{1,5},{2,6},{3,7},{4,0},{5,1},{6,2},{7,3},{8,12},{9,13},{10,... | collective-permute-start | bytes 1179656 | tf_op jit(solution)/shard_map/ppermute | solution.py:24
  159.6 77.2 %slice-start = ((s8[8388608]{0:T(1024)(128)(4,1)}), s8[4194304]{0:T(1024)(128)(4,1)S(1)}, s32[]{:S(2)}) async-start(s8[8388608]{0:T(1024)(128)(4,1)} %bitcast.142), calls=%async_computation | async-start | bytes 8388608
  176.4 46.3 %collective-permute-start.35 = (bf16[256,768]{1,0:T(8,128)(2,1)S(1)}, bf16[256,768]{1,0:T(8,128)(2,1)}, u32[]{:S(2)}, u32[]{:S(2)}) collective-permute-start(bf16[256,768]{1,0:T(8,128)(2,1)S(1)} %copy-done.17), channel_id=1, source_target_pairs={{0,4},{1,5},{2,6},{3,7},{4,0},{5,1},{6,2},{7,3},{8,12},{9,13},{10,... | collective-permute-start | bytes 1179656 | tf_op jit(solution)/shard_map/ppermute | solution.py:24
  193.2 37.2 %collective-permute-start.38 = (bf16[256,768]{1,0:T(8,128)(2,1)S(1)}, bf16[256,768]{1,0:T(8,128)(2,1)}, u32[]{:S(2)}, u32[]{:S(2)}) collective-permute-start(bf16[256,768]{1,0:T(8,128)(2,1)S(1)} %copy-done.16), channel_id=1, source_target_pairs={{0,4},{1,5},{2,6},{3,7},{4,0},{5,1},{6,2},{7,3},{8,12},{9,13},{10,... | collective-permute-start | bytes 1179656 | tf_op jit(solution)/shard_map/ppermute | solution.py:24
  210.1 24.4 %collective-permute-start.41 = (bf16[256,768]{1,0:T(8,128)(2,1)S(1)}, bf16[256,768]{1,0:T(8,128)(2,1)S(1)}, u32[]{:S(2)}, u32[]{:S(2)}) collective-permute-start(bf16[256,768]{1,0:T(8,128)(2,1)S(1)} %get-tuple-element.18), channel_id=1, source_target_pairs={{0,4},{1,5},{2,6},{3,7},{4,0},{5,1},{6,2},{7,3},{8,12},{9,13},{10,... | collective-permute-start | bytes 1179656 | tf_op jit(solution)/shard_map/ppermute | solution.py:24
  222.8 23.7 %collective-permute-start.44 = (bf16[2048,256]{1,0:T(8,128)(2,1)S(1)}, bf16[2048,256]{1,0:T(8,128)(2,1)S(1)}, u32[]{:S(2)}, u32[]{:S(2)}) collective-permute-start(bf16[2048,256]{1,0:T(8,128)(2,1)S(1)} %slice.97.refs_4_), channel_id=1, source_target_pairs={{0,16},{8,24},{16,0},{24,8},{1,17},{9,25},{17,1},{25,9},{2,18},{10... | collective-permute-start | bytes 3145736 | tf_op jit(solution)/shard_map/ppermute | solution.py:24
  230.4 12.6 %collective-permute-start.21 = (bf16[256,768]{1,0:T(8,128)(2,1)}, bf16[256,768]{1,0:T(8,128)(2,1)S(1)}, u32[]{:S(2)}, u32[]{:S(2)}) collective-permute-start(bf16[256,768]{1,0:T(8,128)(2,1)} %collective-permute-done.20), channel_id=1, source_target_pairs={{0,1},{1,0},{2,3},{3,2},{4,5},{5,4},{6,7},{7,6},{8,9},{9,8},{10,11... | collective-permute-start | bytes 1179656 | tf_op jit(solution)/shard_map/ppermute | solution.py:18
  234.5 34.5 %collective-permute-start.24 = (bf16[256,768]{1,0:T(8,128)(2,1)}, bf16[256,768]{1,0:T(8,128)(2,1)S(1)}, u32[]{:S(2)}, u32[]{:S(2)}) collective-permute-start(bf16[256,768]{1,0:T(8,128)(2,1)} %collective-permute-done.23), channel_id=1, source_target_pairs={{0,1},{1,0},{2,3},{3,2},{4,5},{5,4},{6,7},{7,6},{8,9},{9,8},{10,11... | collective-permute-start | bytes 1179656 | tf_op jit(solution)/shard_map/ppermute | solution.py:18
  236.3 8.9 %collective-permute-start.27 = (bf16[256,768]{1,0:T(8,128)(2,1)}, bf16[256,768]{1,0:T(8,128)(2,1)S(1)}, u32[]{:S(2)}, u32[]{:S(2)}) collective-permute-start(bf16[256,768]{1,0:T(8,128)(2,1)} %collective-permute-done.26), channel_id=1, source_target_pairs={{0,1},{1,0},{2,3},{3,2},{4,5},{5,4},{6,7},{7,6},{8,9},{9,8},{10,11... | collective-permute-start | bytes 1179656 | tf_op jit(solution)/shard_map/ppermute | solution.py:18
  243.0 14.2 %collective-permute-start.30 = (bf16[256,768]{1,0:T(8,128)(2,1)S(1)}, bf16[256,768]{1,0:T(8,128)(2,1)S(1)}, u32[]{:S(2)}, u32[]{:S(2)}) collective-permute-start(bf16[256,768]{1,0:T(8,128)(2,1)S(1)} %collective-permute-done.29), channel_id=1, source_target_pairs={{0,1},{1,0},{2,3},{3,2},{4,5},{5,4},{6,7},{7,6},{8,9},{9,8},{10,11... | collective-permute-start | bytes 1179656 | tf_op jit(solution)/shard_map/ppermute | solution.py:18
  245.2 14.5 %collective-permute-start.33 = (bf16[256,768]{1,0:T(8,128)(2,1)S(1)}, bf16[256,768]{1,0:T(8,128)(2,1)S(1)}, u32[]{:S(2)}, u32[]{:S(2)}) collective-permute-start(bf16[256,768]{1,0:T(8,128)(2,1)S(1)} %collective-permute-done.32), channel_id=1, source_target_pairs={{0,1},{1,0},{2,3},{3,2},{4,5},{5,4},{6,7},{7,6},{8,9},{9,8},{10,11... | collective-permute-start | bytes 1179656 | tf_op jit(solution)/shard_map/ppermute | solution.py:18
  246.6 15.9 %collective-permute-start.36 = (bf16[256,768]{1,0:T(8,128)(2,1)}, bf16[256,768]{1,0:T(8,128)(2,1)S(1)}, u32[]{:S(2)}, u32[]{:S(2)}) collective-permute-start(bf16[256,768]{1,0:T(8,128)(2,1)} %collective-permute-done.35), channel_id=1, source_target_pairs={{0,1},{1,0},{2,3},{3,2},{4,5},{5,4},{6,7},{7,6},{8,9},{9,8},{10,11... | collective-permute-start | bytes 1179656 | tf_op jit(solution)/shard_map/ppermute | solution.py:18
  246.6 17.1 %collective-permute-start.39 = (bf16[256,768]{1,0:T(8,128)(2,1)}, bf16[256,768]{1,0:T(8,128)(2,1)}, u32[]{:S(2)}, u32[]{:S(2)}) collective-permute-start(bf16[256,768]{1,0:T(8,128)(2,1)} %collective-permute-done.38), channel_id=1, source_target_pairs={{0,1},{1,0},{2,3},{3,2},{4,5},{5,4},{6,7},{7,6},{8,9},{9,8},{10,11... | collective-permute-start | bytes 1179656 | tf_op jit(solution)/shard_map/ppermute | solution.py:18
  257.3 48.7 %collective-permute-start.46 = (bf16[2,1024,256]{2,1,0:T(8,128)(2,1)}, bf16[2,1024,256]{2,1,0:T(8,128)(2,1)S(1)}, u32[]{:S(2)}, u32[]{:S(2)}) collective-permute-start(bf16[2,1024,256]{2,1,0:T(8,128)(2,1)} %accumulate.3.refs_9_), channel_id=1, source_target_pairs={{0,4},{1,5},{2,6},{3,7},{4,0},{5,1},{6,2},{7,3},{8,12},{9,13},{10,... | collective-permute-start | bytes 3145736 | tf_op jit(solution)/shard_map/ppermute | solution.py:24
  259.8 10.6 %collective-permute-start.42 = (bf16[256,768]{1,0:T(8,128)(2,1)S(1)}, bf16[256,768]{1,0:T(8,128)(2,1)S(1)}, u32[]{:S(2)}, u32[]{:S(2)}) collective-permute-start(bf16[256,768]{1,0:T(8,128)(2,1)S(1)} %collective-permute-done.41), channel_id=1, source_target_pairs={{0,1},{1,0},{2,3},{3,2},{4,5},{5,4},{6,7},{7,6},{8,9},{9,8},{10,11... | collective-permute-start | bytes 1179656 | tf_op jit(solution)/shard_map/ppermute | solution.py:18
  262.4 46.8 %copy-start.8 = (bf16[256,1024]{1,0:T(8,128)(2,1)}, bf16[256,1024]{1,0:T(8,128)(2,1)S(1)}, u32[]{:S(2)}) copy-start(bf16[256,1024]{1,0:T(8,128)(2,1)S(1)} %fusion.171.refs_8_) | copy-start | bytes 1572868
  262.4 43.5 %copy-start.22 = (f32[1024,256]{0,1:T(8,128)S(1)}, f32[1024,256]{0,1:T(8,128)}, u32[]{:S(2)}) copy-start(f32[1024,256]{0,1:T(8,128)} %fusion.26) | copy-start | bytes 3145732
  262.5 14.9 %collective-permute-start.28 = (bf16[256,1024]{1,0:T(8,128)(2,1)S(1)}, bf16[256,1024]{1,0:T(8,128)(2,1)S(1)}, u32[]{:S(2)}, u32[]{:S(2)}) collective-permute-start(bf16[256,1024]{1,0:T(8,128)(2,1)S(1)} %fusion.177.refs_4_), channel_id=1, source_target_pairs={{0,16},{8,24},{16,0},{24,8},{1,17},{9,25},{17,1},{25,9},{2,18},{10... | collective-permute-start | bytes 1572872 | tf_op jit(solution)/shard_map/ppermute | solution.py:24
  263.8 24.8 %collective-permute-start.31 = (bf16[256,1024]{1,0:T(8,128)(2,1)S(1)}, bf16[256,1024]{1,0:T(8,128)(2,1)S(1)}, u32[]{:S(2)}, u32[]{:S(2)}) collective-permute-start(bf16[256,1024]{1,0:T(8,128)(2,1)S(1)} %fusion.174.refs_6_), channel_id=1, source_target_pairs={{0,16},{8,24},{16,0},{24,8},{1,17},{9,25},{17,1},{25,9},{2,18},{10... | collective-permute-start | bytes 1572872 | tf_op jit(solution)/shard_map/ppermute | solution.py:24
  266.6 45.5 %copy-start.11 = (bf16[256,1024]{1,0:T(8,128)(2,1)}, bf16[256,1024]{1,0:T(8,128)(2,1)S(1)}, u32[]{:S(2)}) copy-start(bf16[256,1024]{1,0:T(8,128)(2,1)S(1)} %fusion.168.refs_10_) | copy-start | bytes 1572868
  266.6 42.6 %copy-start.23 = (f32[1024,256]{0,1:T(8,128)S(1)}, f32[1024,256]{0,1:T(8,128)}, u32[]{:S(2)}) copy-start(f32[1024,256]{0,1:T(8,128)} %fusion.30) | copy-start | bytes 3145732
  269.0 44.5 %copy-start.12 = (bf16[256,1024]{1,0:T(8,128)(2,1)}, bf16[256,1024]{1,0:T(8,128)(2,1)S(1)}, u32[]{:S(2)}) copy-start(bf16[256,1024]{1,0:T(8,128)(2,1)S(1)} %fusion.165.refs_12_) | copy-start | bytes 1572868
  269.0 43.1 %collective-permute-start.34 = (bf16[256,1024]{1,0:T(8,128)(2,1)S(1)}, bf16[256,1024]{1,0:T(8,128)(2,1)S(1)}, u32[]{:S(2)}, u32[]{:S(2)}) collective-permute-start(bf16[256,1024]{1,0:T(8,128)(2,1)S(1)} %fusion.171.refs_8_), channel_id=1, source_target_pairs={{0,16},{8,24},{16,0},{24,8},{1,17},{9,25},{17,1},{25,9},{2,18},{10... | collective-permute-start | bytes 1572872 | tf_op jit(solution)/shard_map/ppermute | solution.py:24
  270.4 43.1 %collective-permute-start.37 = (bf16[256,1024]{1,0:T(8,128)(2,1)S(1)}, bf16[256,1024]{1,0:T(8,128)(2,1)S(1)}, u32[]{:S(2)}, u32[]{:S(2)}) collective-permute-start(bf16[256,1024]{1,0:T(8,128)(2,1)S(1)} %fusion.168.refs_10_), channel_id=1, source_target_pairs={{0,16},{8,24},{16,0},{24,8},{1,17},{9,25},{17,1},{25,9},{2,18},{10... | collective-permute-start | bytes 1572872 | tf_op jit(solution)/shard_map/ppermute | solution.py:24
  277.3 44.9 %collective-permute-start.40 = (bf16[256,1024]{1,0:T(8,128)(2,1)S(1)}, bf16[256,1024]{1,0:T(8,128)(2,1)S(1)}, u32[]{:S(2)}, u32[]{:S(2)}) collective-permute-start(bf16[256,1024]{1,0:T(8,128)(2,1)S(1)} %fusion.165.refs_12_), channel_id=1, source_target_pairs={{0,16},{8,24},{16,0},{24,8},{1,17},{9,25},{17,1},{25,9},{2,18},{10... | collective-permute-start | bytes 1572872 | tf_op jit(solution)/shard_map/ppermute | solution.py:24
  288.6 66.8 %collective-permute-start.45 = (bf16[2,1024,256]{2,1,0:T(8,128)(2,1)S(1)}, bf16[2,1024,256]{2,1,0:T(8,128)(2,1)S(1)}, u32[]{:S(2)}, u32[]{:S(2)}) collective-permute-start(bf16[2,1024,256]{2,1,0:T(8,128)(2,1)S(1)} %copy-done), channel_id=1, source_target_pairs={{0,1},{1,0},{2,3},{3,2},{4,5},{5,4},{6,7},{7,6},{8,9},{9,8},{10,11... | collective-permute-start | bytes 3145736 | tf_op jit(solution)/shard_map/ppermute | solution.py:18
  306.0 47.4 %copy-start.2 = (bf16[2,1024,256]{2,1,0:T(8,128)(2,1)}, bf16[2,1024,256]{2,1,0:T(8,128)(2,1)S(1)}, u32[]{:S(2)}) copy-start(bf16[2,1024,256]{2,1,0:T(8,128)(2,1)S(1)} %collective-permute-done.46.refs_11_) | copy-start | bytes 3145732
  306.0 49.4 %collective-permute-start.47 = (bf16[2,1024,256]{2,1,0:T(8,128)(2,1)S(1)}, bf16[2,1024,256]{2,1,0:T(8,128)(2,1)}, u32[]{:S(2)}, u32[]{:S(2)}) collective-permute-start(bf16[2,1024,256]{2,1,0:T(8,128)(2,1)S(1)} %collective-permute-done.46.refs_11_), channel_id=1, source_target_pairs={{0,1},{1,0},{2,3},{3,2},{4,5},{5,4},{6,7},{7,6},{8,9},{9,8},{10,11... | collective-permute-start | bytes 3145736 | tf_op jit(solution)/shard_map/ppermute | solution.py:18
  312.2 21.5 %collective-permute-start.43 = (bf16[256,1024]{1,0:T(8,128)(2,1)}, bf16[256,1024]{1,0:T(8,128)(2,1)}, u32[]{:S(2)}, u32[]{:S(2)}) collective-permute-start(bf16[256,1024]{1,0:T(8,128)(2,1)} %fusion.186.refs_14_), channel_id=1, source_target_pairs={{0,16},{8,24},{16,0},{24,8},{1,17},{9,25},{17,1},{25,9},{2,18},{10... | collective-permute-start | bytes 1572872 | tf_op jit(solution)/shard_map/ppermute | solution.py:24
  313.5 39.9 %collective-permute-start.22 = (bf16[256,1024]{1,0:T(8,128)(2,1)}, bf16[256,1024]{1,0:T(8,128)(2,1)}, u32[]{:S(2)}, u32[]{:S(2)}) collective-permute-start(bf16[256,1024]{1,0:T(8,128)(2,1)} %fusion.183.refs_4_), channel_id=1, source_target_pairs={{0,16},{8,24},{16,0},{24,8},{1,17},{9,25},{17,1},{25,9},{2,18},{10... | collective-permute-start | bytes 1572872 | tf_op jit(solution)/shard_map/ppermute | solution.py:24
  323.1 32.3 %collective-permute-start.25 = (bf16[256,1024]{1,0:T(8,128)(2,1)}, bf16[256,1024]{1,0:T(8,128)(2,1)}, u32[]{:S(2)}, u32[]{:S(2)}) collective-permute-start(bf16[256,1024]{1,0:T(8,128)(2,1)} %fusion.180.refs_6_), channel_id=1, source_target_pairs={{0,16},{8,24},{16,0},{24,8},{1,17},{9,25},{17,1},{25,9},{2,18},{10... | collective-permute-start | bytes 1572872 | tf_op jit(solution)/shard_map/ppermute | solution.py:24
  375.2 2.0 collective-permute-start.48
  378.6 7.9 %collective-permute-start.51 = (bf16[256,256]{1,0:T(8,128)(2,1)S(1)}, bf16[256,256]{1,0:T(8,128)(2,1)S(1)}, u32[]{:S(2)}, u32[]{:S(2)}) collective-permute-start(bf16[256,256]{1,0:T(8,128)(2,1)S(1)} %get-tuple-element.33), channel_id=1, source_target_pairs={{0,6},{1,7},{2,4},{3,5},{4,2},{5,3},{6,0},{7,1},{8,14},{9,15},{10,... | collective-permute-start | bytes 393224 | tf_op jit(solution)/shard_map/ppermute | solution.py:18
  381.9 12.5 %collective-permute-start.50 = (bf16[256,256]{1,0:T(8,128)(2,1)S(1)}, bf16[256,256]{1,0:T(8,128)(2,1)S(1)}, u32[]{:S(2)}, u32[]{:S(2)}) collective-permute-start(bf16[256,256]{1,0:T(8,128)(2,1)S(1)} %get-tuple-element.34), channel_id=1, source_target_pairs={{0,4},{1,5},{2,6},{3,7},{4,0},{5,1},{6,2},{7,3},{8,12},{9,13},{10,... | collective-permute-start | bytes 393224 | tf_op jit(solution)/shard_map/ppermute | solution.py:18
  383.9 10.5 %collective-permute-start.49 = (bf16[256,256]{1,0:T(8,128)(2,1)S(1)}, bf16[256,256]{1,0:T(8,128)(2,1)S(1)}, u32[]{:S(2)}, u32[]{:S(2)}) collective-permute-start(bf16[256,256]{1,0:T(8,128)(2,1)S(1)} %get-tuple-element.32), channel_id=1, source_target_pairs={{0,2},{1,3},{2,0},{3,1},{4,6},{5,7},{6,4},{7,5},{8,10},{9,11},{10,... | collective-permute-start | bytes 393224 | tf_op jit(solution)/shard_map/ppermute | solution.py:18
  (16 other events, 256.7 us)
where the time goes:
time: 396 us; the launch traced here: 395 us
  waiting for transfers between devices  200 us (51%)
  starting transfers between devices  61.5 us (16%)
  matrix products  51 us (13%)
  Pallas kernels  46.9 us (12%)
  local copies, waits for them, and re-layouts  27.2 us (7%)
  other arithmetic  6.88 us (2%)
    ppermute x18, waiting for transfers between devices, shifted(): return lax.ppermute(value, axis, pairs)  140 us
    dot_general x18, matrix products, dot(): return jnp.dot(a, b, preferred_element_type=jnp.float32)  51 us
    ppermute x6, waiting for transfers between devices, gathered_block(): downs.append(lax.ppermute(downs[-1], 'col', down_pairs))  32.7 us
    pallas_call x2, Pallas kernels, accumulate(): pl.pallas_call(body, out_shape=jax.ShapeDtypeStruct((2, tall, wide), dtyp...  29.5 us
    ppermute x22, waiting for transfers between devices, flipped(): return lax.ppermute(value, axis, pairs)  27.3 us
    ppermute x18, starting transfers between devices, shifted(): return lax.ppermute(value, axis, pairs)  23.5 us
    pallas_call x1, Pallas kernels, finish(): pl.pallas_call(body, out_shape=(jax.ShapeDtypeStruct((2 * tall, wide), jn...  17.4 us
    ppermute x22, starting transfers between devices, flipped(): return lax.ppermute(value, axis, pairs)  16.4 us
  transfers between devices with their start and end apart: 52, of which 27 were waited for; matrix products, arithmetic and copies ran while one was open for 19% of the time, Pallas kernels for 7%

commit v1 on v0

--- a/solution.py
+++ b/solution.py
@@ -1,3 +1,5 @@
+import math
+
 import jax
 import jax.numpy as jnp
 from jax import lax
@@ -8,7 +10,7 @@
 
 decay_factor = 0.8
 parts = (2,) * 8
-groups = ((0, 6),)
+groups = ((0, 2), (2, 7))
 first_quarters = 3
 pieces = 2
 
@@ -50,12 +52,13 @@
 
 def tile_product(refs, kept, h, start):
     b_own, b_par, perm, scale = refs
+    b_own, b_par = [jnp.concatenate([one[...] for one in b]) for b in (b_own, b_par)]
     near, far = kept
     shape = (perm.shape[1], near.shape[0])
     index = start + lax.broadcasted_iota(jnp.int32, shape, 1)
     chosen = (index == perm[0]).astype(jnp.bfloat16)
     moved = dot(chosen, far[...]) * scale[0]
-    return moved + dot_t(jnp.where(h == 0, b_own[...], b_par[...]), near[...])
+    return moved + dot_t(jnp.where(h == 0, b_own, b_par), near[...])
 
 
 def keep(chunks, kept):
@@ -72,9 +75,17 @@
 def tile_specs(start, depth, chunks, tile, tiles, at):
     wide = chunks[0][0].shape[1]
     last = at(tiles - 1)
-    specs = [
-        pl.BlockSpec((depth, tile), lambda h, i, *_: (start // depth, jnp.where(h == 0, at(i), last))),
-        pl.BlockSpec((depth, tile), lambda h, i, *_: (start // depth, jnp.where(h == 0, at(0), at(i)))),
+    unit = math.gcd(start, depth)
+    blocks = range(start // unit, (start + depth) // unit)
+
+    def own(block):
+        return lambda h, i, *_: (block, jnp.where(h == 0, at(i), last))
+
+    def par(block):
+        return lambda h, i, *_: (block, jnp.where(h == 0, at(0), at(i)))
+
+    specs = [pl.BlockSpec((unit, tile), place(block)) for place in (own, par) for block in blocks]
+    specs += [
         pl.BlockSpec((1, tile, 1), lambda h, i, *_: (h, at(i), 0)),
         pl.BlockSpec((1, tile, 1), lambda h, i, *_: (h, at(i), 0)),
     ]
@@ -98,18 +109,21 @@
     tile = min(512, tall)
     count = len(chunks)
 
+    blocks = depth // math.gcd(start, depth)
+
     def body(*refs):
+        b, refs = (refs[:blocks], refs[blocks : 2 * blocks]), refs[2 * blocks :]
         kept = refs[-2:]
         out = refs[-3]
-        keep(paired(refs[4:], count), kept)
-        result = tile_product(refs[:4], kept, pl.program_id(0), start)
+        keep(paired(refs[2:], count), kept)
+        result = tile_product((*b, *refs[:2]), kept, pl.program_id(0), start)
         if total is not None:
             result = result + refs[-4][0]
         out[0] = result.astype(dtype)
 
     place = pl.BlockSpec((1, tile, wide), lambda h, i: (h, i, 0))
     specs = tile_specs(start, depth, chunks, tile, tall // tile, lambda i: i)
-    operands = [*halves, perm, scale, *flat(chunks)]
+    operands = [*[halves[0]] * blocks, *[halves[1]] * blocks, perm, scale, *flat(chunks)]
     if total is not None:
         specs.append(place)
         operands.append(total)
@@ -135,10 +149,13 @@
     thin = late[0].shape[2]
     width = features.shape[1]
 
+    blocks = depth // math.gcd(start, depth)
+
     def body(origin_ref, *refs):
         h = pl.program_id(0)
-        keep(paired(refs[4:], count), refs[-2:])
-        others = refs[4 + 2 * count :]
+        b, refs = (refs[:blocks], refs[blocks : 2 * blocks]), refs[2 * blocks :]
+        keep(paired(refs[2:], count), refs[-2:])
+        others = refs[2 + 2 * count :]
         total_ref, here, here_par, there, there_par = others[:5]
         b_own, b_par, perm_c, scale_c, feature_ref, sim_ref, sum_ref = others[5:12]
         index = lax.broadcasted_iota(jnp.int32, (thin, wide), 0)
@@ -147,7 +164,7 @@
         moved = dot(there[0], g_own) + dot(there_par[0], g_par)
         result = total_ref[0] + moved * scale_c[...]
         result = result + dot(here[0], b_own[...]) + dot(here_par[0], b_par[...])
-        result = result + tile_product(refs[:4], refs[-2:], h, start)
+        result = result + tile_product((*b, *refs[:2]), refs[-2:], h, start)
         place = jnp.where(h == 0, origin_ref[0], 1 - origin_ref[0])
         row = origin_ref[1] + place * tall + pl.program_id(1) * tile
         row = row + lax.broadcasted_iota(jnp.int32, result.shape, 0)
@@ -181,7 +198,10 @@
         ),
         compiler_params=pltpu.CompilerParams(vmem_limit_bytes=58 * 2**20),
         name="finish",
-    )(origin, *halves, perm, scale, *flat(chunks), total, *late, *arrived, *fixed)
+    )(
+        origin, *[halves[0]] * blocks, *[halves[1]] * blocks, perm, scale, *flat(chunks),
+        total, *late, *arrived, *fixed,
+    )
 
 
 def gathered_block(diag_blocks, row_id, block_id, row_count, block_count):

time: 396 us -> 401 us (1.013)
  Pallas kernels: 46.9 us -> 52.2 us
    pallas_call x2 -> x3, Pallas kernels: 29.5 us -> 37.2 us  [accumulate(): pl.pallas_call(body, out_shape=jax.ShapeDtypeStruct((2, tall, wide), dtyp...]
  transfers between devices with their start and end apart: 52 -> 52, of which waited for: 27 -> 26; matrix products, arithmetic and copies ran while one was open for 19% -> 19% of each run, Pallas kernels for 7% -> 9%
where the time goes in v1:
time: 401 us; the launch traced here: 400 us
  waiting for transfers between devices  201 us (50%)
  starting transfers between devices  61.5 us (15%)
  Pallas kernels  52.2 us (13%)
  matrix products  50.2 us (13%)
  local copies, waits for them, and re-layouts  27.2 us (7%)
  other arithmetic  6.88 us (2%)
    ppermute x18, waiting for transfers between devices, shifted(): return lax.ppermute(value, axis, pairs)  141 us
    dot_general x18, matrix products, dot(): return jnp.dot(a, b, preferred_element_type=jnp.float32)  50.2 us
    pallas_call x3, Pallas kernels, accumulate(): pl.pallas_call(body, out_shape=jax.ShapeDtypeStruct((2, tall, wide), dtyp...  37.2 us
    ppermute x6, waiting for transfers between devices, gathered_block(): downs.append(lax.ppermute(downs[-1], 'col', down_pairs))  32.7 us
    ppermute x22, waiting for transfers between devices, flipped(): return lax.ppermute(value, axis, pairs)  27.3 us
    ppermute x18, starting transfers between devices, shifted(): return lax.ppermute(value, axis, pairs)  23.5 us
    ppermute x22, starting transfers between devices, flipped(): return lax.ppermute(value, axis, pairs)  16.4 us
    pallas_call x1, Pallas kernels, finish(): pl.pallas_call(body, out_shape=(jax.ShapeDtypeStruct((2 * tall, wide), jn...  15 us
  transfers between devices with their start and end apart: 52, of which 26 were waited for; matrix products, arithmetic and copies ran while one was open for 19% of the time, Pallas kernels for 9%

profile of v1, /device:TPU:0, one launch (start us, length us, event | category | flops | bytes accessed | tf_op | source)
XLA Modules:
  0.0 400.1 jit_solution(13091612520942803413)
XLA Ops:
  0.7 2.7 constant_dynamic-slice_fusion
  4.7 5.6 %collective-permute-start = (bf16[256,1024]{1,0:T(8,128)(2,1)S(1)}, bf16[256,1024]{1,0:T(8,128)(2,1)S(1)}, u32[]{:S(2)}, u32[]{:S(2)}) collective-permute-start(bf16[256,1024]{1,0:T(8,128)(2,1)S(1)} %get-tuple-element.16), channel_id=1, source_target_pairs={{0,2},{1,3},{2,4},{3,5},{4,6},{5,7},{8,10},{9,11},{10,12},{11,13},... | collective-permute-start | bytes 1572872 | tf_op jit(solution)/shard_map/ppermute | solution.py:219
  11.6 4.6 %collective-permute-start.6 = (bf16[256,1024]{1,0:T(8,128)(2,1)S(1)}, bf16[256,1024]{1,0:T(8,128)(2,1)S(1)}, u32[]{:S(2)}, u32[]{:S(2)}) collective-permute-start(bf16[256,1024]{1,0:T(8,128)(2,1)S(1)} %get-tuple-element.15), channel_id=1, source_target_pairs={{0,2},{1,3},{2,4},{3,5},{4,6},{5,7},{8,10},{9,11},{10,12},{11,13},... | collective-permute-start | bytes 1572872 | tf_op jit(solution)/shard_map/ppermute | solution.py:219
  16.2 4.9 %collective-permute-done.3 = bf16[256,1024]{1,0:T(8,128)(2,1)S(1)} collective-permute-done((bf16[256,1024]{1,0:T(8,128)(2,1)S(1)}, bf16[256,1024]{1,0:T(8,128)(2,1)S(1)}, u32[]{:S(2)}, u32[]{:S(2)}) %collective-permute-start.3) | collective-permute-done | bytes 524320 | tf_op jit(solution)/shard_map/ppermute | solution.py:220
  22.6 1.5 collective-permute-start.1
  24.1 8.3 %collective-permute-done.9 = bf16[256,1024]{1,0:T(8,128)(2,1)S(1)} collective-permute-done((bf16[256,1024]{1,0:T(8,128)(2,1)S(1)}, bf16[256,1024]{1,0:T(8,128)(2,1)S(1)}, u32[]{:S(2)}, u32[]{:S(2)}) %collective-permute-start.9) | collective-permute-done | bytes 524320 | tf_op jit(solution)/shard_map/ppermute | solution.py:220
  34.4 9.3 %collective-permute-done.4 = bf16[256,1024]{1,0:T(8,128)(2,1)} collective-permute-done((bf16[256,1024]{1,0:T(8,128)(2,1)S(1)}, bf16[256,1024]{1,0:T(8,128)(2,1)}, u32[]{:S(2)}, u32[]{:S(2)}) %collective-permute-start.4) | collective-permute-done | bytes 524320 | tf_op jit(solution)/shard_map/ppermute | solution.py:220
  45.7 9.2 %fusion.33 = f32[1024,2048]{0,1:T(8,128)} fusion(bf16[2048,1024]{1,0:T(8,128)(2,1)} %param.5, bf16[2048,1024]{1,0:T(8,128)(2,1)} %param.6, s32[]{:T(128)S(6)} %select_n.294), kind=kOutput, calls=%fused_computation.34 | convolution fusion | flops 3221225472 | bytes 13107204 | tf_op jit(solution)/shard_map/dot_general | solution.py:30
  57.0 9.0 %collective-permute-done.5 = bf16[256,1024]{1,0:T(8,128)(2,1)S(1)} collective-permute-done((bf16[256,1024]{1,0:T(8,128)(2,1)}, bf16[256,1024]{1,0:T(8,128)(2,1)S(1)}, u32[]{:S(2)}, u32[]{:S(2)}) %collective-permute-start.5) | collective-permute-done | bytes 524320 | tf_op jit(solution)/shard_map/ppermute | solution.py:220
  66.1 1.6 select_select_fusion.3
  67.6 2.6 broadcast_in_dim.10
  70.2 1.7 select_select_fusion.4
  71.9 1.9 collective-permute-start.12
  73.8 1.5 collective-permute-start.13
  76.5 2.6 collective-permute-start.14
  81.1 3.5 fusion.197
  84.6 2.3 collective-permute-done.12
  87.0 1.9 collective-permute-start.16
  89.9 7.9 %collective-permute-done.13 = bf16[256,1024]{1,0:T(8,128)(2,1)} collective-permute-done((bf16[256,1024]{1,0:T(8,128)(2,1)}, bf16[256,1024]{1,0:T(8,128)(2,1)}, u32[]{:S(2)}, u32[]{:S(2)}) %collective-permute-start.13) | collective-permute-done | bytes 524320 | tf_op jit(solution)/shard_map/ppermute | solution.py:20
  98.5 1.9 constant_dynamic-update-slice_fusion.5
  100.4 1.9 constant_dynamic-update-slice_fusion.4
  102.3 4.9 %collective-permute-start.20 = (bf16[256,768]{1,0:T(8,128)(2,1)}, bf16[256,768]{1,0:T(8,128)(2,1)}, u32[]{:S(2)}, u32[]{:S(2)}) collective-permute-start(bf16[256,768]{1,0:T(8,128)(2,1)} %get-tuple-element.25), channel_id=1, source_target_pairs={{0,4},{1,5},{2,6},{3,7},{4,0},{5,1},{6,2},{7,3},{8,12},{9,13},{10,... | collective-permute-start | bytes 1179656 | tf_op jit(solution)/shard_map/ppermute | solution.py:26
  107.2 1.9 constant_dynamic-update-slice_fusion.3
  109.4 4.6 %collective-permute-start.23 = (bf16[256,768]{1,0:T(8,128)(2,1)}, bf16[256,768]{1,0:T(8,128)(2,1)}, u32[]{:S(2)}, u32[]{:S(2)}) collective-permute-start(bf16[256,768]{1,0:T(8,128)(2,1)} %get-tuple-element.24), channel_id=1, source_target_pairs={{0,4},{1,5},{2,6},{3,7},{4,0},{5,1},{6,2},{7,3},{8,12},{9,13},{10,... | collective-permute-start | bytes 1179656 | tf_op jit(solution)/shard_map/ppermute | solution.py:26
  114.8 4.3 %collective-permute-done.16 = bf16[256,1024]{1,0:T(8,128)(2,1)S(1)} collective-permute-done((bf16[256,1024]{1,0:T(8,128)(2,1)S(1)}, bf16[256,1024]{1,0:T(8,128)(2,1)S(1)}, u32[]{:S(2)}, u32[]{:S(2)}) %collective-permute-start.16) | collective-permute-done | bytes 524320 | tf_op jit(solution)/shard_map/ppermute | solution.py:20
  119.1 3.6 collective-permute-start.26
  129.5 13.3 %collective-permute-done.20 = bf16[256,768]{1,0:T(8,128)(2,1)} collective-permute-done((bf16[256,768]{1,0:T(8,128)(2,1)}, bf16[256,768]{1,0:T(8,128)(2,1)}, u32[]{:S(2)}, u32[]{:S(2)}) %collective-permute-start.20) | collective-permute-done | bytes 393248 | tf_op jit(solution)/shard_map/ppermute | solution.py:26
  142.7 1.8 fusion.28
  144.5 15.1 %collective-permute-done.23 = bf16[256,768]{1,0:T(8,128)(2,1)} collective-permute-done((bf16[256,768]{1,0:T(8,128)(2,1)}, bf16[256,768]{1,0:T(8,128)(2,1)}, u32[]{:S(2)}, u32[]{:S(2)}) %collective-permute-start.23) | collective-permute-done | bytes 393248 | tf_op jit(solution)/shard_map/ppermute | solution.py:26
  159.6 1.9 fusion.26
  161.5 14.9 %collective-permute-done.26 = bf16[256,768]{1,0:T(8,128)(2,1)} collective-permute-done((bf16[256,768]{1,0:T(8,128)(2,1)}, bf16[256,768]{1,0:T(8,128)(2,1)}, u32[]{:S(2)}, u32[]{:S(2)}) %collective-permute-start.26) | collective-permute-done | bytes 393248 | tf_op jit(solution)/shard_map/ppermute | solution.py:26
  176.5 2.7 fusion.24
  179.2 14.0 %collective-permute-done.29 = bf16[256,768]{1,0:T(8,128)(2,1)S(1)} collective-permute-done((bf16[256,768]{1,0:T(8,128)(2,1)}, bf16[256,768]{1,0:T(8,128)(2,1)S(1)}, u32[]{:S(2)}, u32[]{:S(2)}) %collective-permute-start.29) | collective-permute-done | bytes 393248 | tf_op jit(solution)/shard_map/ppermute | solution.py:26
  193.2 1.8 fusion.22
  195.0 15.1 %collective-permute-done.32 = bf16[256,768]{1,0:T(8,128)(2,1)S(1)} collective-permute-done((bf16[256,768]{1,0:T(8,128)(2,1)S(1)}, bf16[256,768]{1,0:T(8,128)(2,1)S(1)}, u32[]{:S(2)}, u32[]{:S(2)}) %collective-permute-start.32) | collective-permute-done | bytes 393248 | tf_op jit(solution)/shard_map/ppermute | solution.py:26
  210.1 1.8 fusion.20
  211.8 11.0 %collective-permute-done.35 = bf16[256,768]{1,0:T(8,128)(2,1)} collective-permute-done((bf16[256,768]{1,0:T(8,128)(2,1)S(1)}, bf16[256,768]{1,0:T(8,128)(2,1)}, u32[]{:S(2)}, u32[]{:S(2)}) %collective-permute-start.35) | collective-permute-done | bytes 393248 | tf_op jit(solution)/shard_map/ppermute | solution.py:26
  224.2 2.8 fusion.18
  227.1 3.2 collective-permute-done.38
  230.3 1.8 fusion.16
  232.1 2.4 collective-permute-done.41
  234.5 1.8 fusion.30
  236.8 6.2 %add_bitcast_fusion = f32[2048,1024]{1,0:T(8,128)S(1)} fusion(f32[1024,2048]{0,1:T(8,128)S(1)} %bitcast.143, bf16[2048,1024]{1,0:T(8,128)(2,1)} %collective-permute-done.19, bf16[2048,1024]{1,0:T(8,128)(2,1)} %param.6, s32[]{:T(128)S(6)} %select_n.296), kind=kOutput, calls=%fused_computation.32 | convolution fusion | flops 3223322624 | bytes 21495812 | tf_op jit(solution)/shard_map/dot_general | solution.py:30
  243.0 2.1 fusion.183.refs_4_
  247.5 9.7 %accumulate.5.refs_7_ = bf16[2,1024,256]{2,1,0:T(8,128)(2,1)} custom-call(bf16[2048,1024]{1,0:T(8,128)(2,1)} %constant_dynamic-update-slice_fusion.refs_0_.refs_1_.refs_2_.refs_3_.refs_4_, bf16[2048,1024]{1,0:T(8,128)(2,1)} %collective-permute-done.18.refs_1_.refs_5_.refs_6_.refs_7_.refs_8_.refs_9_, s32[2,1024,1]{2,1,0:T(8,128)} %copy.51.refs_2_.refs_10_, ...), custom_call_target="tpu_custom_call" | custom-call | tf_op jit(solution)/shard_map/accumulate/pallas_call | solution.py:130
  257.3 2.4 fusion.177.refs_14_
  259.8 2.6 fusion.174.refs_16_
  264.5 2.2 fusion.165.refs_4_
  266.7 2.4 fusion.186.refs_6_
  271.2 6.1 %collective-permute-done.25.refs_13_ = bf16[256,1024]{1,0:T(8,128)(2,1)S(1)} collective-permute-done((bf16[256,1024]{1,0:T(8,128)(2,1)S(1)}, bf16[256,1024]{1,0:T(8,128)(2,1)S(1)}, u32[]{:S(2)}, u32[]{:S(2)}) %collective-permute-start.25) | collective-permute-done | bytes 524320 | tf_op jit(solution)/shard_map/ppermute | solution.py:26
  278.5 10.0 %collective-permute-done.28.refs_15_ = bf16[256,1024]{1,0:T(8,128)(2,1)S(1)} collective-permute-done((bf16[256,1024]{1,0:T(8,128)(2,1)S(1)}, bf16[256,1024]{1,0:T(8,128)(2,1)S(1)}, u32[]{:S(2)}, u32[]{:S(2)}) %collective-permute-start.28) | collective-permute-done | bytes 524320 | tf_op jit(solution)/shard_map/ppermute | solution.py:26
  288.5 17.4 %collective-permute-done.46.refs_9_ = bf16[2,1024,256]{2,1,0:T(8,128)(2,1)S(1)} collective-permute-done((bf16[2,1024,256]{2,1,0:T(8,128)(2,1)}, bf16[2,1024,256]{2,1,0:T(8,128)(2,1)S(1)}, u32[]{:S(2)}, u32[]{:S(2)}) %collective-permute-start.46) | collective-permute-done | bytes 1048608 | tf_op jit(solution)/shard_map/ppermute | solution.py:26
  305.9 3.2 fusion.171.refs_18_
  309.2 2.9 fusion.168.refs_20_
  314.3 7.9 %collective-permute-done.43.refs_7_ = bf16[256,1024]{1,0:T(8,128)(2,1)S(1)} collective-permute-done((bf16[256,1024]{1,0:T(8,128)(2,1)S(1)}, bf16[256,1024]{1,0:T(8,128)(2,1)S(1)}, u32[]{:S(2)}, u32[]{:S(2)}) %collective-permute-start.43) | collective-permute-done | bytes 524320 | tf_op jit(solution)/shard_map/ppermute | solution.py:26
  324.9 9.6 %accumulate.3.refs_22_ = f32[2,1024,1024]{2,1,0:T(8,128)} custom-call(bf16[2048,1024]{1,0:T(8,128)(2,1)} %constant_dynamic-update-slice_fusion.refs_0_.refs_1_.refs_2_.refs_3_.refs_4_, bf16[2048,1024]{1,0:T(8,128)(2,1)} %collective-permute-done.18.refs_1_.refs_5_.refs_6_.refs_7_.refs_8_.refs_9_, s32[2,1024,1]{2,1,0:T(8,128)} %copy.51.refs_2_.refs_10_, ...), custom_call_target="tpu_custom_call" | custom-call | tf_op jit(solution)/shard_map/accumulate/pallas_call | solution.py:130
  334.5 10.3 %collective-permute-done.37.refs_21_ = bf16[256,1024]{1,0:T(8,128)(2,1)} collective-permute-done((bf16[256,1024]{1,0:T(8,128)(2,1)}, bf16[256,1024]{1,0:T(8,128)(2,1)}, u32[]{:S(2)}, u32[]{:S(2)}) %collective-permute-start.37) | collective-permute-done | bytes 524320 | tf_op jit(solution)/shard_map/ppermute | solution.py:26
  344.8 17.9 %accumulate.4.refs_6_ = f32[2,1024,1024]{2,1,0:T(8,128)} custom-call(bf16[2048,1024]{1,0:T(8,128)(2,1)} %constant_dynamic-update-slice_fusion.refs_0_.refs_1_.refs_2_.refs_3_.refs_4_, bf16[2048,1024]{1,0:T(8,128)(2,1)} %constant_dynamic-update-slice_fusion.refs_0_.refs_1_.refs_2_.refs_3_.refs_4_, ...), custom_call_target="tpu_custom_call", output_to_operand_aliasing={{}: (22, {})} | custom-call | tf_op jit(solution)/shard_map/accumulate/pallas_call | solution.py:130
  363.8 15.0 %finish.1 = (bf16[2048,1024]{1,0:T(8,128)(2,1)}, f32[2048,256]{1,0:T(8,128)}) custom-call(s32[5]{0:T(128)} %stack.33.origin_ref, bf16[2048,1024]{1,0:T(8,128)(2,1)} %constant_dynamic-update-slice_fusion.refs_0_.refs_1_.refs_2_.refs_3_.refs_4_, bf16[2048,1024]{1,0:T(8,128)(2,1)} %collective-permute-done.18.refs_1_.refs_5_.refs_6_.refs_7_.refs_8_.refs_9_, ...), custom_call_target="tpu_custom_call" | custom-call | tf_op jit(solution)/shard_map/finish/pallas_call | solution.py:186
  380.2 1.9 collective-permute-done.48
  383.5 3.3 collective-permute-start.51
  386.8 1.9 collective-permute-start.50
  388.8 2.6 collective-permute-done.51
  391.4 7.9 %collective-permute-done.50 = bf16[256,256]{1,0:T(8,128)(2,1)S(1)} collective-permute-done((bf16[256,256]{1,0:T(8,128)(2,1)S(1)}, bf16[256,256]{1,0:T(8,128)(2,1)S(1)}, u32[]{:S(2)}, u32[]{:S(2)}) %collective-permute-start.50) | collective-permute-done | bytes 131104 | tf_op jit(solution)/shard_map/ppermute | solution.py:20
  (146 shorter events, 42.3 us)
Async XLA Ops:
  3.4 17.7 %collective-permute-start.3 = (bf16[256,1024]{1,0:T(8,128)(2,1)S(1)}, bf16[256,1024]{1,0:T(8,128)(2,1)S(1)}, u32[]{:S(2)}, u32[]{:S(2)}) collective-permute-start(bf16[256,1024]{1,0:T(8,128)(2,1)S(1)} %get-tuple-element.16), channel_id=1, source_target_pairs={{2,0},{3,1},{4,2},{5,3},{6,4},{7,5},{10,8},{11,9},{12,10},{13,11},... | collective-permute-start | bytes 1572872 | tf_op jit(solution)/shard_map/ppermute | solution.py:220
  4.7 17.9 %collective-permute-start = (bf16[256,1024]{1,0:T(8,128)(2,1)S(1)}, bf16[256,1024]{1,0:T(8,128)(2,1)S(1)}, u32[]{:S(2)}, u32[]{:S(2)}) collective-permute-start(bf16[256,1024]{1,0:T(8,128)(2,1)S(1)} %get-tuple-element.16), channel_id=1, source_target_pairs={{0,2},{1,3},{2,4},{3,5},{4,6},{5,7},{8,10},{9,11},{10,12},{11,13},... | collective-permute-start | bytes 1572872 | tf_op jit(solution)/shard_map/ppermute | solution.py:219
  10.3 22.0 %collective-permute-start.9 = (bf16[256,1024]{1,0:T(8,128)(2,1)S(1)}, bf16[256,1024]{1,0:T(8,128)(2,1)S(1)}, u32[]{:S(2)}, u32[]{:S(2)}) collective-permute-start(bf16[256,1024]{1,0:T(8,128)(2,1)S(1)} %get-tuple-element.15), channel_id=1, source_target_pairs={{2,0},{3,1},{4,2},{5,3},{6,4},{7,5},{10,8},{11,9},{12,10},{13,11},... | collective-permute-start | bytes 1572872 | tf_op jit(solution)/shard_map/ppermute | solution.py:220
  11.6 22.0 %collective-permute-start.6 = (bf16[256,1024]{1,0:T(8,128)(2,1)S(1)}, bf16[256,1024]{1,0:T(8,128)(2,1)S(1)}, u32[]{:S(2)}, u32[]{:S(2)}) collective-permute-start(bf16[256,1024]{1,0:T(8,128)(2,1)S(1)} %get-tuple-element.15), channel_id=1, source_target_pairs={{0,2},{1,3},{2,4},{3,5},{4,6},{5,7},{8,10},{9,11},{10,12},{11,13},... | collective-permute-start | bytes 1572872 | tf_op jit(solution)/shard_map/ppermute | solution.py:219
  21.1 22.6 %collective-permute-start.4 = (bf16[256,1024]{1,0:T(8,128)(2,1)S(1)}, bf16[256,1024]{1,0:T(8,128)(2,1)}, u32[]{:S(2)}, u32[]{:S(2)}) collective-permute-start(bf16[256,1024]{1,0:T(8,128)(2,1)S(1)} %collective-permute-done.3), channel_id=1, source_target_pairs={{2,0},{3,1},{4,2},{5,3},{10,8},{11,9},{12,10},{13,11},{18,16},{19,... | collective-permute-start | bytes 1572872 | tf_op jit(solution)/shard_map/ppermute | solution.py:220
  22.6 22.4 %collective-permute-start.1 = (bf16[256,1024]{1,0:T(8,128)(2,1)S(1)}, bf16[256,1024]{1,0:T(8,128)(2,1)}, u32[]{:S(2)}, u32[]{:S(2)}) collective-permute-start(bf16[256,1024]{1,0:T(8,128)(2,1)S(1)} %collective-permute-done), channel_id=1, source_target_pairs={{2,4},{3,5},{4,6},{5,7},{10,12},{11,13},{12,14},{13,15},{18,20},{1... | collective-permute-start | bytes 1572872 | tf_op jit(solution)/shard_map/ppermute | solution.py:219
  24.1 212.2 %collective-permute-start.19 = (bf16[2048,1024]{1,0:T(8,128)(2,1)}, bf16[2048,1024]{1,0:T(8,128)(2,1)}, u32[]{:S(2)}, u32[]{:S(2)}) collective-permute-start(bf16[2048,1024]{1,0:T(8,128)(2,1)} %param.5), channel_id=1, source_target_pairs={{0,1},{1,0},{2,3},{3,2},{4,5},{5,4},{6,7},{7,6},{8,9},{9,8},{10,11... | collective-permute-start | bytes 12582920 | tf_op jit(solution)/shard_map/ppermute | solution.py:20
  32.4 22.5 %collective-permute-start.10 = (bf16[256,1024]{1,0:T(8,128)(2,1)S(1)}, bf16[256,1024]{1,0:T(8,128)(2,1)S(1)}, u32[]{:S(2)}, u32[]{:S(2)}) collective-permute-start(bf16[256,1024]{1,0:T(8,128)(2,1)S(1)} %collective-permute-done.9), channel_id=1, source_target_pairs={{2,0},{3,1},{4,2},{5,3},{10,8},{11,9},{12,10},{13,11},{18,16},{19,... | collective-permute-start | bytes 1572872 | tf_op jit(solution)/shard_map/ppermute | solution.py:220
  33.7 22.5 %collective-permute-start.7 = (bf16[256,1024]{1,0:T(8,128)(2,1)S(1)}, bf16[256,1024]{1,0:T(8,128)(2,1)S(1)}, u32[]{:S(2)}, u32[]{:S(2)}) collective-permute-start(bf16[256,1024]{1,0:T(8,128)(2,1)S(1)} %collective-permute-done.6), channel_id=1, source_target_pairs={{2,4},{3,5},{4,6},{5,7},{10,12},{11,13},{12,14},{13,15},{18,20},{1... | collective-permute-start | bytes 1572872 | tf_op jit(solution)/shard_map/ppermute | solution.py:219
  43.7 22.4 %collective-permute-start.5 = (bf16[256,1024]{1,0:T(8,128)(2,1)}, bf16[256,1024]{1,0:T(8,128)(2,1)S(1)}, u32[]{:S(2)}, u32[]{:S(2)}) collective-permute-start(bf16[256,1024]{1,0:T(8,128)(2,1)} %collective-permute-done.4), channel_id=1, source_target_pairs={{2,0},{3,1},{10,8},{11,9},{18,16},{19,17},{26,24},{27,25}} | collective-permute-start | bytes 1572872 | tf_op jit(solution)/shard_map/ppermute | solution.py:220
  45.0 21.1 %collective-permute-start.2 = (bf16[256,1024]{1,0:T(8,128)(2,1)}, bf16[256,1024]{1,0:T(8,128)(2,1)S(1)}, u32[]{:S(2)}, u32[]{:S(2)}) collective-permute-start(bf16[256,1024]{1,0:T(8,128)(2,1)} %collective-permute-done.1), channel_id=1, source_target_pairs={{4,6},{5,7},{12,14},{13,15},{20,22},{21,23},{28,30},{29,31}} | collective-permute-start | bytes 1572872 | tf_op jit(solution)/shard_map/ppermute | solution.py:219
  54.9 21.6 %collective-permute-start.11 = (bf16[256,1024]{1,0:T(8,128)(2,1)S(1)}, bf16[256,1024]{1,0:T(8,128)(2,1)S(1)}, u32[]{:S(2)}, u32[]{:S(2)}) collective-permute-start(bf16[256,1024]{1,0:T(8,128)(2,1)S(1)} %collective-permute-done.10), channel_id=1, source_target_pairs={{2,0},{3,1},{10,8},{11,9},{18,16},{19,17},{26,24},{27,25}} | collective-permute-start | bytes 1572872 | tf_op jit(solution)/shard_map/ppermute | solution.py:220
  56.2 22.9 %collective-permute-start.8 = (bf16[256,1024]{1,0:T(8,128)(2,1)S(1)}, bf16[256,1024]{1,0:T(8,128)(2,1)S(1)}, u32[]{:S(2)}, u32[]{:S(2)}) collective-permute-start(bf16[256,1024]{1,0:T(8,128)(2,1)S(1)} %collective-permute-done.7), channel_id=1, source_target_pairs={{4,6},{5,7},{12,14},{13,15},{20,22},{21,23},{28,30},{29,31}} | collective-permute-start | bytes 1572872 | tf_op jit(solution)/shard_map/ppermute | solution.py:219
  71.9 15.1 %collective-permute-start.12 = (bf16[256,1024]{1,0:T(8,128)(2,1)}, bf16[256,1024]{1,0:T(8,128)(2,1)}, u32[]{:S(2)}, u32[]{:S(2)}) collective-permute-start(bf16[256,1024]{1,0:T(8,128)(2,1)} %get-tuple-element.30), channel_id=1, source_target_pairs={{0,8},{8,0},{16,24},{24,16},{1,9},{9,1},{17,25},{25,17},{2,10},{10... | collective-permute-start | bytes 1572872 | tf_op jit(solution)/shard_map/ppermute | solution.py:20
  73.8 24.0 %collective-permute-start.13 = (bf16[256,1024]{1,0:T(8,128)(2,1)}, bf16[256,1024]{1,0:T(8,128)(2,1)}, u32[]{:S(2)}, u32[]{:S(2)}) collective-permute-start(bf16[256,1024]{1,0:T(8,128)(2,1)} %get-tuple-element.29), channel_id=1, source_target_pairs={{0,16},{8,24},{16,0},{24,8},{1,17},{9,25},{17,1},{25,9},{2,18},{10... | collective-permute-start | bytes 1572872 | tf_op jit(solution)/shard_map/ppermute | solution.py:20
  76.5 25.8 %collective-permute-start.14 = (bf16[256,1024]{1,0:T(8,128)(2,1)S(1)}, bf16[256,1024]{1,0:T(8,128)(2,1)}, u32[]{:S(2)}, u32[]{:S(2)}) collective-permute-start(bf16[256,1024]{1,0:T(8,128)(2,1)S(1)} %get-tuple-element.10), channel_id=1, source_target_pairs={{0,24},{8,16},{16,8},{24,0},{1,25},{9,17},{17,9},{25,1},{2,26},{10... | collective-permute-start | bytes 1572872 | tf_op jit(solution)/shard_map/ppermute | solution.py:20
  80.6 28.8 %collective-permute-start.15 = (bf16[256,1024]{1,0:T(8,128)(2,1)S(1)}, bf16[256,1024]{1,0:T(8,128)(2,1)S(1)}, u32[]{:S(2)}, u32[]{:S(2)}) collective-permute-start(bf16[256,1024]{1,0:T(8,128)(2,1)S(1)} %get-tuple-element.27), channel_id=1, source_target_pairs={{0,8},{8,0},{16,24},{24,16},{1,9},{9,1},{17,25},{25,17},{2,10},{10... | collective-permute-start | bytes 1572872 | tf_op jit(solution)/shard_map/ppermute | solution.py:20
  87.0 32.1 %collective-permute-start.16 = (bf16[256,1024]{1,0:T(8,128)(2,1)S(1)}, bf16[256,1024]{1,0:T(8,128)(2,1)S(1)}, u32[]{:S(2)}, u32[]{:S(2)}) collective-permute-start(bf16[256,1024]{1,0:T(8,128)(2,1)S(1)} %get-tuple-element.26), channel_id=1, source_target_pairs={{0,16},{8,24},{16,0},{24,8},{1,17},{9,25},{17,1},{25,9},{2,18},{10... | collective-permute-start | bytes 1572872 | tf_op jit(solution)/shard_map/ppermute | solution.py:20
  89.8 219.3 %copy-start.19 = (s32[1,1024]{1,0:T(1,128)}, s32[1,1024]{1,0:T(1,128)S(1)}, u32[]{:S(2)}) copy-start(s32[1,1024]{1,0:T(1,128)S(1)} %get-tuple-element.38.refs_13_) | copy-start | bytes 12292
  97.8 25.8 %collective-permute-start.17 = (bf16[256,1024]{1,0:T(8,128)(2,1)S(1)}, bf16[256,1024]{1,0:T(8,128)(2,1)S(1)}, u32[]{:S(2)}, u32[]{:S(2)}) collective-permute-start(bf16[256,1024]{1,0:T(8,128)(2,1)S(1)} %get-tuple-element.6), channel_id=1, source_target_pairs={{0,24},{8,16},{16,8},{24,0},{1,25},{9,17},{17,9},{25,1},{2,26},{10... | collective-permute-start | bytes 1572872 | tf_op jit(solution)/shard_map/ppermute | solution.py:20
  102.3 40.4 %collective-permute-start.20 = (bf16[256,768]{1,0:T(8,128)(2,1)}, bf16[256,768]{1,0:T(8,128)(2,1)}, u32[]{:S(2)}, u32[]{:S(2)}) collective-permute-start(bf16[256,768]{1,0:T(8,128)(2,1)} %get-tuple-element.25), channel_id=1, source_target_pairs={{0,4},{1,5},{2,6},{3,7},{4,0},{5,1},{6,2},{7,3},{8,12},{9,13},{10,... | collective-permute-start | bytes 1179656 | tf_op jit(solution)/shard_map/ppermute | solution.py:26
  109.4 50.2 %collective-permute-start.23 = (bf16[256,768]{1,0:T(8,128)(2,1)}, bf16[256,768]{1,0:T(8,128)(2,1)}, u32[]{:S(2)}, u32[]{:S(2)}) collective-permute-start(bf16[256,768]{1,0:T(8,128)(2,1)} %get-tuple-element.24), channel_id=1, source_target_pairs={{0,4},{1,5},{2,6},{3,7},{4,0},{5,1},{6,2},{7,3},{8,12},{9,13},{10,... | collective-permute-start | bytes 1179656 | tf_op jit(solution)/shard_map/ppermute | solution.py:26
  119.1 40.5 %copy-start.18 = (bf16[256,768]{1,0:T(8,128)(2,1)S(1)}, bf16[256,768]{1,0:T(8,128)(2,1)}, u32[]{:S(2)}) copy-start(bf16[256,768]{1,0:T(8,128)(2,1)} %get-tuple-element.21) | copy-start | bytes 1179652
  119.1 57.4 %collective-permute-start.26 = (bf16[256,768]{1,0:T(8,128)(2,1)}, bf16[256,768]{1,0:T(8,128)(2,1)}, u32[]{:S(2)}, u32[]{:S(2)}) collective-permute-start(bf16[256,768]{1,0:T(8,128)(2,1)} %get-tuple-element.23), channel_id=1, source_target_pairs={{0,4},{1,5},{2,6},{3,7},{4,0},{5,1},{6,2},{7,3},{8,12},{9,13},{10,... | collective-permute-start | bytes 1179656 | tf_op jit(solution)/shard_map/ppermute | solution.py:26
  124.4 122.2 %collective-permute-start.18 = (bf16[2048,1024]{1,0:T(8,128)(2,1)}, bf16[2048,1024]{1,0:T(8,128)(2,1)}, u32[]{:S(2)}, u32[]{:S(2)}) collective-permute-start(bf16[2048,1024]{1,0:T(8,128)(2,1)} %constant_dynamic-update-slice_fusion.refs_0_.refs_1_.refs_2_.refs_3_.refs_4_), channel_id=1, source_target_pairs={{0,1},{1,0},{2,3},{3,2},{4,5},{5,4},{6,7},{7,6},{8,9},{9,8},{10,11... | collective-permute-start | bytes 12582920 | tf_op jit(solution)/shard_map/ppermute | solution.py:20
  125.3 183.8 %copy-start.20 = (f32[1,1024]{1,0:T(1,128)}, f32[1,1024]{1,0:T(1,128)S(1)}, u32[]{:S(2)}) copy-start(f32[1,1024]{1,0:T(1,128)S(1)} %get-tuple-element.35.refs_14_) | copy-start | bytes 12292
  125.4 51.1 %copy-start.17 = (bf16[256,768]{1,0:T(8,128)(2,1)S(1)}, bf16[256,768]{1,0:T(8,128)(2,1)}, u32[]{:S(2)}) copy-start(bf16[256,768]{1,0:T(8,128)(2,1)} %get-tuple-element.20) | copy-start | bytes 1179652
  126.7 96.1 %copy-start = (bf16[2048,256]{1,0:T(8,128)(2,1)}, bf16[2048,256]{1,0:T(8,128)(2,1)S(1)}, u32[]{:S(2)}) copy-start(bf16[2048,256]{1,0:T(8,128)(2,1)S(1)} %slice.97.refs_4_) | copy-start | bytes 3145732
  128.1 65.1 %copy-start.16 = (bf16[256,768]{1,0:T(8,128)(2,1)S(1)}, bf16[256,768]{1,0:T(8,128)(2,1)}, u32[]{:S(2)}) copy-start(bf16[256,768]{1,0:T(8,128)(2,1)} %get-tuple-element.19) | copy-start | bytes 1179652
  142.7 50.5 %collective-permute-start.29 = (bf16[256,768]{1,0:T(8,128)(2,1)}, bf16[256,768]{1,0:T(8,128)(2,1)S(1)}, u32[]{:S(2)}, u32[]{:S(2)}) collective-permute-start(bf16[256,768]{1,0:T(8,128)(2,1)} %get-tuple-element.22), channel_id=1, source_target_pairs={{0,4},{1,5},{2,6},{3,7},{4,0},{5,1},{6,2},{7,3},{8,12},{9,13},{10,... | collective-permute-start | bytes 1179656 | tf_op jit(solution)/shard_map/ppermute | solution.py:26
  159.6 50.5 %collective-permute-start.32 = (bf16[256,768]{1,0:T(8,128)(2,1)S(1)}, bf16[256,768]{1,0:T(8,128)(2,1)S(1)}, u32[]{:S(2)}, u32[]{:S(2)}) collective-permute-start(bf16[256,768]{1,0:T(8,128)(2,1)S(1)} %copy-done.18), channel_id=1, source_target_pairs={{0,4},{1,5},{2,6},{3,7},{4,0},{5,1},{6,2},{7,3},{8,12},{9,13},{10,... | collective-permute-start | bytes 1179656 | tf_op jit(solution)/shard_map/ppermute | solution.py:26
  159.6 77.2 %slice-start = ((s8[8388608]{0:T(1024)(128)(4,1)}), s8[4194304]{0:T(1024)(128)(4,1)S(1)}, s32[]{:S(2)}) async-start(s8[8388608]{0:T(1024)(128)(4,1)} %bitcast.142), calls=%async_computation | async-start | bytes 8388608
  176.4 46.3 %collective-permute-start.35 = (bf16[256,768]{1,0:T(8,128)(2,1)S(1)}, bf16[256,768]{1,0:T(8,128)(2,1)}, u32[]{:S(2)}, u32[]{:S(2)}) collective-permute-start(bf16[256,768]{1,0:T(8,128)(2,1)S(1)} %copy-done.17), channel_id=1, source_target_pairs={{0,4},{1,5},{2,6},{3,7},{4,0},{5,1},{6,2},{7,3},{8,12},{9,13},{10,... | collective-permute-start | bytes 1179656 | tf_op jit(solution)/shard_map/ppermute | solution.py:26
  193.2 37.1 %collective-permute-start.38 = (bf16[256,768]{1,0:T(8,128)(2,1)S(1)}, bf16[256,768]{1,0:T(8,128)(2,1)S(1)}, u32[]{:S(2)}, u32[]{:S(2)}) collective-permute-start(bf16[256,768]{1,0:T(8,128)(2,1)S(1)} %copy-done.16), channel_id=1, source_target_pairs={{0,4},{1,5},{2,6},{3,7},{4,0},{5,1},{6,2},{7,3},{8,12},{9,13},{10,... | collective-permute-start | bytes 1179656 | tf_op jit(solution)/shard_map/ppermute | solution.py:26
  210.1 24.4 %collective-permute-start.41 = (bf16[256,768]{1,0:T(8,128)(2,1)S(1)}, bf16[256,768]{1,0:T(8,128)(2,1)S(1)}, u32[]{:S(2)}, u32[]{:S(2)}) collective-permute-start(bf16[256,768]{1,0:T(8,128)(2,1)S(1)} %get-tuple-element.18), channel_id=1, source_target_pairs={{0,4},{1,5},{2,6},{3,7},{4,0},{5,1},{6,2},{7,3},{8,12},{9,13},{10,... | collective-permute-start | bytes 1179656 | tf_op jit(solution)/shard_map/ppermute | solution.py:26
  222.8 23.7 %collective-permute-start.44 = (bf16[2048,256]{1,0:T(8,128)(2,1)S(1)}, bf16[2048,256]{1,0:T(8,128)(2,1)S(1)}, u32[]{:S(2)}, u32[]{:S(2)}) collective-permute-start(bf16[2048,256]{1,0:T(8,128)(2,1)S(1)} %slice.97.refs_4_), channel_id=1, source_target_pairs={{0,16},{8,24},{16,0},{24,8},{1,17},{9,25},{17,1},{25,9},{2,18},{10... | collective-permute-start | bytes 3145736 | tf_op jit(solution)/shard_map/ppermute | solution.py:26
  230.3 12.7 %collective-permute-start.21 = (bf16[256,768]{1,0:T(8,128)(2,1)}, bf16[256,768]{1,0:T(8,128)(2,1)S(1)}, u32[]{:S(2)}, u32[]{:S(2)}) collective-permute-start(bf16[256,768]{1,0:T(8,128)(2,1)} %collective-permute-done.20), channel_id=1, source_target_pairs={{0,1},{1,0},{2,3},{3,2},{4,5},{5,4},{6,7},{7,6},{8,9},{9,8},{10,11... | collective-permute-start | bytes 1179656 | tf_op jit(solution)/shard_map/ppermute | solution.py:20
  234.5 10.7 %collective-permute-start.24 = (bf16[256,768]{1,0:T(8,128)(2,1)}, bf16[256,768]{1,0:T(8,128)(2,1)S(1)}, u32[]{:S(2)}, u32[]{:S(2)}) collective-permute-start(bf16[256,768]{1,0:T(8,128)(2,1)} %collective-permute-done.23), channel_id=1, source_target_pairs={{0,1},{1,0},{2,3},{3,2},{4,5},{5,4},{6,7},{7,6},{8,9},{9,8},{10,11... | collective-permute-start | bytes 1179656 | tf_op jit(solution)/shard_map/ppermute | solution.py:20
  236.2 20.9 %collective-permute-start.27 = (bf16[256,768]{1,0:T(8,128)(2,1)}, bf16[256,768]{1,0:T(8,128)(2,1)S(1)}, u32[]{:S(2)}, u32[]{:S(2)}) collective-permute-start(bf16[256,768]{1,0:T(8,128)(2,1)} %collective-permute-done.26), channel_id=1, source_target_pairs={{0,1},{1,0},{2,3},{3,2},{4,5},{5,4},{6,7},{7,6},{8,9},{9,8},{10,11... | collective-permute-start | bytes 1179656 | tf_op jit(solution)/shard_map/ppermute | solution.py:20
  242.9 16.7 %collective-permute-start.30 = (bf16[256,768]{1,0:T(8,128)(2,1)S(1)}, bf16[256,768]{1,0:T(8,128)(2,1)S(1)}, u32[]{:S(2)}, u32[]{:S(2)}) collective-permute-start(bf16[256,768]{1,0:T(8,128)(2,1)S(1)} %collective-permute-done.29), channel_id=1, source_target_pairs={{0,1},{1,0},{2,3},{3,2},{4,5},{5,4},{6,7},{7,6},{8,9},{9,8},{10,11... | collective-permute-start | bytes 1179656 | tf_op jit(solution)/shard_map/ppermute | solution.py:20
  245.2 23.9 %collective-permute-start.33 = (bf16[256,768]{1,0:T(8,128)(2,1)S(1)}, bf16[256,768]{1,0:T(8,128)(2,1)S(1)}, u32[]{:S(2)}, u32[]{:S(2)}) collective-permute-start(bf16[256,768]{1,0:T(8,128)(2,1)S(1)} %collective-permute-done.32), channel_id=1, source_target_pairs={{0,1},{1,0},{2,3},{3,2},{4,5},{5,4},{6,7},{7,6},{8,9},{9,8},{10,11... | collective-permute-start | bytes 1179656 | tf_op jit(solution)/shard_map/ppermute | solution.py:20
  246.5 15.9 %collective-permute-start.39 = (bf16[256,768]{1,0:T(8,128)(2,1)S(1)}, bf16[256,768]{1,0:T(8,128)(2,1)}, u32[]{:S(2)}, u32[]{:S(2)}) collective-permute-start(bf16[256,768]{1,0:T(8,128)(2,1)S(1)} %collective-permute-done.38), channel_id=1, source_target_pairs={{0,1},{1,0},{2,3},{3,2},{4,5},{5,4},{6,7},{7,6},{8,9},{9,8},{10,11... | collective-permute-start | bytes 1179656 | tf_op jit(solution)/shard_map/ppermute | solution.py:20
  246.6 17.1 %collective-permute-start.42 = (bf16[256,768]{1,0:T(8,128)(2,1)S(1)}, bf16[256,768]{1,0:T(8,128)(2,1)}, u32[]{:S(2)}, u32[]{:S(2)}) collective-permute-start(bf16[256,768]{1,0:T(8,128)(2,1)S(1)} %collective-permute-done.41), channel_id=1, source_target_pairs={{0,1},{1,0},{2,3},{3,2},{4,5},{5,4},{6,7},{7,6},{8,9},{9,8},{10,11... | collective-permute-start | bytes 1179656 | tf_op jit(solution)/shard_map/ppermute | solution.py:20
  257.2 48.7 %collective-permute-start.46 = (bf16[2,1024,256]{2,1,0:T(8,128)(2,1)}, bf16[2,1024,256]{2,1,0:T(8,128)(2,1)S(1)}, u32[]{:S(2)}, u32[]{:S(2)}) collective-permute-start(bf16[2,1024,256]{2,1,0:T(8,128)(2,1)} %accumulate.5.refs_7_), channel_id=1, source_target_pairs={{0,4},{1,5},{2,6},{3,7},{4,0},{5,1},{6,2},{7,3},{8,12},{9,13},{10,... | collective-permute-start | bytes 3145736 | tf_op jit(solution)/shard_map/ppermute | solution.py:26
  259.7 10.7 %collective-permute-start.36 = (bf16[256,768]{1,0:T(8,128)(2,1)}, bf16[256,768]{1,0:T(8,128)(2,1)S(1)}, u32[]{:S(2)}, u32[]{:S(2)}) collective-permute-start(bf16[256,768]{1,0:T(8,128)(2,1)} %collective-permute-done.35), channel_id=1, source_target_pairs={{0,1},{1,0},{2,3},{3,2},{4,5},{5,4},{6,7},{7,6},{8,9},{9,8},{10,11... | collective-permute-start | bytes 1179656 | tf_op jit(solution)/shard_map/ppermute | solution.py:20
  262.3 46.8 %copy-start.7 = (bf16[256,1024]{1,0:T(8,128)(2,1)}, bf16[256,1024]{1,0:T(8,128)(2,1)S(1)}, u32[]{:S(2)}) copy-start(bf16[256,1024]{1,0:T(8,128)(2,1)S(1)} %fusion.174.refs_16_) | copy-start | bytes 1572868
  262.4 43.5 %copy-start.22 = (f32[1024,256]{0,1:T(8,128)S(1)}, f32[1024,256]{0,1:T(8,128)}, u32[]{:S(2)}) copy-start(f32[1024,256]{0,1:T(8,128)} %fusion.20) | copy-start | bytes 3145732
  262.4 14.9 %collective-permute-start.25 = (bf16[256,1024]{1,0:T(8,128)(2,1)S(1)}, bf16[256,1024]{1,0:T(8,128)(2,1)S(1)}, u32[]{:S(2)}, u32[]{:S(2)}) collective-permute-start(bf16[256,1024]{1,0:T(8,128)(2,1)S(1)} %fusion.180.refs_12_), channel_id=1, source_target_pairs={{0,16},{8,24},{16,0},{24,8},{1,17},{9,25},{17,1},{25,9},{2,18},{10... | collective-permute-start | bytes 1572872 | tf_op jit(solution)/shard_map/ppermute | solution.py:26
  263.7 24.8 %collective-permute-start.28 = (bf16[256,1024]{1,0:T(8,128)(2,1)S(1)}, bf16[256,1024]{1,0:T(8,128)(2,1)S(1)}, u32[]{:S(2)}, u32[]{:S(2)}) collective-permute-start(bf16[256,1024]{1,0:T(8,128)(2,1)S(1)} %fusion.177.refs_14_), channel_id=1, source_target_pairs={{0,16},{8,24},{16,0},{24,8},{1,17},{9,25},{17,1},{25,9},{2,18},{10... | collective-permute-start | bytes 1572872 | tf_op jit(solution)/shard_map/ppermute | solution.py:26
  266.6 45.4 %copy-start.12 = (bf16[256,1024]{1,0:T(8,128)(2,1)}, bf16[256,1024]{1,0:T(8,128)(2,1)S(1)}, u32[]{:S(2)}) copy-start(bf16[256,1024]{1,0:T(8,128)(2,1)S(1)} %fusion.165.refs_4_) | copy-start | bytes 1572868
  266.7 42.5 %copy-start.23 = (f32[1024,256]{0,1:T(8,128)S(1)}, f32[1024,256]{0,1:T(8,128)}, u32[]{:S(2)}) copy-start(f32[1024,256]{0,1:T(8,128)} %fusion.18) | copy-start | bytes 3145732
  269.1 45.2 %copy-start.13 = (bf16[256,1024]{1,0:T(8,128)(2,1)}, bf16[256,1024]{1,0:T(8,128)(2,1)S(1)}, u32[]{:S(2)}) copy-start(bf16[256,1024]{1,0:T(8,128)(2,1)S(1)} %fusion.186.refs_6_) | copy-start | bytes 1572868
  269.1 43.0 %collective-permute-start.31 = (bf16[256,1024]{1,0:T(8,128)(2,1)S(1)}, bf16[256,1024]{1,0:T(8,128)(2,1)S(1)}, u32[]{:S(2)}, u32[]{:S(2)}) collective-permute-start(bf16[256,1024]{1,0:T(8,128)(2,1)S(1)} %fusion.174.refs_16_), channel_id=1, source_target_pairs={{0,16},{8,24},{16,0},{24,8},{1,17},{9,25},{17,1},{25,9},{2,18},{10... | collective-permute-start | bytes 1572872 | tf_op jit(solution)/shard_map/ppermute | solution.py:26
  270.4 43.0 %collective-permute-start.40 = (bf16[256,1024]{1,0:T(8,128)(2,1)S(1)}, bf16[256,1024]{1,0:T(8,128)(2,1)S(1)}, u32[]{:S(2)}, u32[]{:S(2)}) collective-permute-start(bf16[256,1024]{1,0:T(8,128)(2,1)S(1)} %fusion.165.refs_4_), channel_id=1, source_target_pairs={{0,16},{8,24},{16,0},{24,8},{1,17},{9,25},{17,1},{25,9},{2,18},{10... | collective-permute-start | bytes 1572872 | tf_op jit(solution)/shard_map/ppermute | solution.py:26
  277.2 44.9 %collective-permute-start.43 = (bf16[256,1024]{1,0:T(8,128)(2,1)S(1)}, bf16[256,1024]{1,0:T(8,128)(2,1)S(1)}, u32[]{:S(2)}, u32[]{:S(2)}) collective-permute-start(bf16[256,1024]{1,0:T(8,128)(2,1)S(1)} %fusion.186.refs_6_), channel_id=1, source_target_pairs={{0,16},{8,24},{16,0},{24,8},{1,17},{9,25},{17,1},{25,9},{2,18},{10... | collective-permute-start | bytes 1572872 | tf_op jit(solution)/shard_map/ppermute | solution.py:26
  288.5 74.2 %collective-permute-start.45 = (bf16[2,1024,256]{2,1,0:T(8,128)(2,1)S(1)}, bf16[2,1024,256]{2,1,0:T(8,128)(2,1)S(1)}, u32[]{:S(2)}, u32[]{:S(2)}) collective-permute-start(bf16[2,1024,256]{2,1,0:T(8,128)(2,1)S(1)} %copy-done.1), channel_id=1, source_target_pairs={{0,1},{1,0},{2,3},{3,2},{4,5},{5,4},{6,7},{7,6},{8,9},{9,8},{10,11... | collective-permute-start | bytes 3145736 | tf_op jit(solution)/shard_map/ppermute | solution.py:20
  305.9 56.8 %collective-permute-start.47 = (bf16[2,1024,256]{2,1,0:T(8,128)(2,1)S(1)}, bf16[2,1024,256]{2,1,0:T(8,128)(2,1)}, u32[]{:S(2)}, u32[]{:S(2)}) collective-permute-start(bf16[2,1024,256]{2,1,0:T(8,128)(2,1)S(1)} %collective-permute-done.46.refs_9_), channel_id=1, source_target_pairs={{0,1},{1,0},{2,3},{3,2},{4,5},{5,4},{6,7},{7,6},{8,9},{9,8},{10,11... | collective-permute-start | bytes 3145736 | tf_op jit(solution)/shard_map/ppermute | solution.py:20
  312.1 22.4 %collective-permute-start.34 = (bf16[256,1024]{1,0:T(8,128)(2,1)}, bf16[256,1024]{1,0:T(8,128)(2,1)}, u32[]{:S(2)}, u32[]{:S(2)}) collective-permute-start(bf16[256,1024]{1,0:T(8,128)(2,1)} %fusion.171.refs_18_), channel_id=1, source_target_pairs={{0,16},{8,24},{16,0},{24,8},{1,17},{9,25},{17,1},{25,9},{2,18},{10... | collective-permute-start | bytes 1572872 | tf_op jit(solution)/shard_map/ppermute | solution.py:26
  313.4 31.3 %collective-permute-start.37 = (bf16[256,1024]{1,0:T(8,128)(2,1)}, bf16[256,1024]{1,0:T(8,128)(2,1)}, u32[]{:S(2)}, u32[]{:S(2)}) collective-permute-start(bf16[256,1024]{1,0:T(8,128)(2,1)} %fusion.168.refs_20_), channel_id=1, source_target_pairs={{0,16},{8,24},{16,0},{24,8},{1,17},{9,25},{17,1},{25,9},{2,18},{10... | collective-permute-start | bytes 1572872 | tf_op jit(solution)/shard_map/ppermute | solution.py:26
  323.0 39.7 %collective-permute-start.22 = (bf16[256,1024]{1,0:T(8,128)(2,1)}, bf16[256,1024]{1,0:T(8,128)(2,1)}, u32[]{:S(2)}, u32[]{:S(2)}) collective-permute-start(bf16[256,1024]{1,0:T(8,128)(2,1)} %fusion.183.refs_4_), channel_id=1, source_target_pairs={{0,16},{8,24},{16,0},{24,8},{1,17},{9,25},{17,1},{25,9},{2,18},{10... | collective-permute-start | bytes 1572872 | tf_op jit(solution)/shard_map/ppermute | solution.py:26
  380.1 2.0 collective-permute-start.48
  383.5 7.9 %collective-permute-start.51 = (bf16[256,256]{1,0:T(8,128)(2,1)S(1)}, bf16[256,256]{1,0:T(8,128)(2,1)S(1)}, u32[]{:S(2)}, u32[]{:S(2)}) collective-permute-start(bf16[256,256]{1,0:T(8,128)(2,1)S(1)} %get-tuple-element.33), channel_id=1, source_target_pairs={{0,6},{1,7},{2,4},{3,5},{4,2},{5,3},{6,0},{7,1},{8,14},{9,15},{10,... | collective-permute-start | bytes 393224 | tf_op jit(solution)/shard_map/ppermute | solution.py:20
  386.8 12.5 %collective-permute-start.50 = (bf16[256,256]{1,0:T(8,128)(2,1)S(1)}, bf16[256,256]{1,0:T(8,128)(2,1)S(1)}, u32[]{:S(2)}, u32[]{:S(2)}) collective-permute-start(bf16[256,256]{1,0:T(8,128)(2,1)S(1)} %get-tuple-element.34), channel_id=1, source_target_pairs={{0,4},{1,5},{2,6},{3,7},{4,0},{5,1},{6,2},{7,3},{8,12},{9,13},{10,... | collective-permute-start | bytes 393224 | tf_op jit(solution)/shard_map/ppermute | solution.py:20
  388.8 10.5 %collective-permute-start.49 = (bf16[256,256]{1,0:T(8,128)(2,1)S(1)}, bf16[256,256]{1,0:T(8,128)(2,1)S(1)}, u32[]{:S(2)}, u32[]{:S(2)}) collective-permute-start(bf16[256,256]{1,0:T(8,128)(2,1)S(1)} %get-tuple-element.32), channel_id=1, source_target_pairs={{0,2},{1,3},{2,0},{3,1},{4,6},{5,7},{6,4},{7,5},{8,10},{9,11},{10,... | collective-permute-start | bytes 393224 | tf_op jit(solution)/shard_map/ppermute | solution.py:20
  (16 other events, 236.4 us)
